TPU v7x, 32 devices: a whole 2x2x4 slice. The times are simulated.
32 devices in a mesh: groups: 2 (over y), tm: 16 (over z, x, core).
Axes of the slice: x: 2, y: 2, z: 4, core: 2. Of those that a mesh axis runs over, the one named last changes fastest.
Arguments:
- frames: bfloat16 [4096, 8192], P('tm', 'groups'), parts along dimension 1, may hold values from -6 to 6
- frame_valid: int32 [8192], P(('groups', 'tm')), parts along dimension 0, may hold values 0 or 1
- valid_count: int32 [32], P('groups'), parts along dimension 0, may hold values from 32 to 128, as said below
- block_map: int32 [32, 256], P('groups'), parts along dimension 0, may hold values from 0 to 255, as said below
- offsets: int32 [4, 2], replicated, may hold values from -4 to 4
Outputs:
- cross: float32 [512, 4, 2, 2048], P(('groups', 'tm')), parts along dimension 0
There are 2 independent parts, one for each index of `groups`. A program takes and returns all parts, laid end to end along the dimension named above; an argument that names none is the same for every part. Nothing has to cross between parts.
Inputs may be any that keep to these rules, and one draw needn't show every extreme that they name: `valid_count`: at most half of a tile's pixels are valid. Some tile has exactly 128 valid pixels and another exactly 32 in every draw; the others are spread evenly between the two. `block_map`: each row is a permutation of the pixels of a tile. Row steps lie in -4 to 4.
All inputs are finite; a program needn't handle non-finite values. No bound on the sum of `frame_valid` on one device may be relied on, other than what follows from the above.
Results may differ from a plain program's by a relative error of at most 0.0052.
Values may be sent and summed in bfloat16 or wider, within the bound.
No kernel may reach another device: no remote copies, remote signals or barrier semaphores. Data moves between devices by JAX's collectives and lax.ppermute only.
A program may use at most 64 MiB of HBM per device.

v0:
```python
import math

import jax
import jax.numpy as jnp
from jax import lax
from jax.sharding import PartitionSpec as P

ROWS = 16
BAND = 256
REACH = 4


def base_angles(frames_len, band_width):
    frame_idx = jnp.arange(frames_len, dtype=jnp.int32)[:, None]
    bin_idx = jnp.arange(band_width, dtype=jnp.int32)[None, :]
    angles = (frame_idx * bin_idx % frames_len).astype(jnp.float32) * (2.0 * math.pi / frames_len)
    return (jnp.cos(angles), jnp.sin(angles))


def rotated_table(base_cos, base_sin, bin_start):
    frames_len = base_cos.shape[0]
    frame_idx = jnp.arange(frames_len, dtype=jnp.int32)
    phase = (frame_idx * bin_start % frames_len).astype(jnp.float32) * (2.0 * math.pi / frames_len)
    phase_cos = jnp.cos(phase)[:, None]
    phase_sin = jnp.sin(phase)[:, None]
    scaling = 1.0 / math.sqrt(frames_len)
    real_part = base_cos * phase_cos - base_sin * phase_sin
    imag_part = -(base_sin * phase_cos + base_cos * phase_sin)
    return (jnp.concatenate([real_part, imag_part], axis=1) * scaling).astype(jnp.bfloat16)


def nearby_validity(valid_count, block_map, position):
    tile_pix = block_map.shape[1]
    padded_count = jnp.pad(valid_count, ((1, 1),))
    padded_map = jnp.pad(block_map, ((1, 1), (0, 0)))
    counts = lax.dynamic_slice_in_dim(padded_count, position, 3, 0)
    slots_map = lax.dynamic_slice_in_dim(padded_map, position, 3, 0)
    slot_idx = jnp.arange(tile_pix, dtype=jnp.int32)
    live = (slot_idx[None, :] < counts[:, None]).astype(jnp.float32)
    match = (slots_map[:, :, None] == slot_idx[None, None, :]).astype(jnp.float32)
    return jnp.sum(live[:, :, None] * match, axis=1)


def transform(columns, table):
    return lax.dot_general(
        columns, table, (((0,), (0,)), ((), ())), preferred_element_type=jnp.float32
    )


def cross_block(extended, ext_valid, offsets, tile_width):
    spectra = extended.astype(jnp.float32)
    row_count = spectra.shape[0]
    half = spectra.shape[2] // 2
    padded = jnp.pad(spectra, ((REACH, REACH), (0, 0), (0, 0)))
    padded_valid = jnp.pad(ext_valid, ((REACH, REACH), (0, 0)))
    own_spec = spectra[:, REACH : REACH + tile_width]
    own_valid = ext_valid[:, REACH : REACH + tile_width]
    own_real = own_spec[..., :half]
    own_imag = own_spec[..., half:]
    results = []
    for which in range(offsets.shape[0]):
        row_step = offsets[which, 0] + REACH
        col_step = offsets[which, 1] + REACH
        shifted = lax.dynamic_slice(
            padded, (row_step, col_step, jnp.int32(0)), (row_count, tile_width, 2 * half)
        )
        shifted_valid = lax.dynamic_slice(
            padded_valid, (row_step, col_step), (row_count, tile_width)
        )
        other_real = shifted[..., :half]
        other_imag = shifted[..., half:]
        real_part = jnp.sum(own_real * other_real + own_imag * other_imag, axis=0)
        imag_part = jnp.sum(own_imag * other_real - own_real * other_imag, axis=0)
        pair_count = jnp.sum(own_valid * shifted_valid, axis=0)
        scaling = 1.0 / jnp.maximum(pair_count, 1.0)
        results.append(jnp.stack([real_part, imag_part], axis=1) * scaling[:, None, None])
    return jnp.stack(results, axis=1)


def per_device(frames, frame_valid, valid_count, block_map, offsets):
    tile_count = lax.axis_size("tm")
    position = lax.axis_index("tm")
    frame_dev, pixel_count = frames.shape
    tile_pix = pixel_count // tile_count
    tile_width = tile_pix // ROWS
    masked = frames * frame_valid[:, None].astype(jnp.bfloat16)
    grouped = masked.reshape(frame_dev, tile_count, tile_pix)
    nearby = nearby_validity(valid_count, block_map, position).reshape(3, ROWS, tile_width)
    ext_valid = jnp.concatenate(
        [nearby[0][:, tile_width - REACH :], nearby[1], nearby[2][:, :REACH]], axis=1
    )
    own_valid = nearby[1].reshape(tile_pix)
    tiled = grouped.reshape(frame_dev, tile_count, ROWS, tile_width)
    blank = jnp.zeros((frame_dev, 1, ROWS, REACH), jnp.bfloat16)
    left_side = jnp.concatenate([blank, tiled[:, :-1, :, tile_width - REACH :]], axis=1)
    right_side = jnp.concatenate([tiled[:, 1:, :, :REACH], blank], axis=1)
    margins = jnp.concatenate([left_side, right_side], axis=3).reshape(
        frame_dev, tile_count, ROWS * 2 * REACH
    )
    tile_frames, margin_frames = (
        lax.all_to_all(grouped, "tm", split_axis=1, concat_axis=0, tiled=True),
        lax.all_to_all(margins, "tm", split_axis=1, concat_axis=0, tiled=True),
    )
    margin_frames = margin_frames.reshape(-1, ROWS * 2 * REACH)
    margin_valid = jnp.concatenate(
        [ext_valid[:, :REACH], ext_valid[:, REACH + tile_width :]], axis=1
    ).reshape(-1)
    tile_frames = tile_frames.reshape(-1, tile_pix)
    frames_len = tile_frames.shape[0]
    bins = frames_len // 2
    base_cos, base_sin = base_angles(frames_len, BAND)

    def own_spectra(table):
        spectra = transform(tile_frames, table) * own_valid[:, None]
        return spectra.astype(jnp.bfloat16).reshape(ROWS, tile_width, table.shape[1])

    def one_band(band_index, result):
        bin_start = (band_index * BAND).astype(jnp.int32)
        table = rotated_table(base_cos, base_sin, bin_start)
        own_spec = own_spectra(table)
        edge_spec = (transform(margin_frames, table) * margin_valid[:, None]).astype(jnp.bfloat16)
        edge_spec = edge_spec.reshape(ROWS, 2 * REACH, table.shape[1])
        extended = jnp.concatenate([edge_spec[:, :REACH], own_spec, edge_spec[:, REACH:]], axis=1)
        band_cross = cross_block(extended, ext_valid, offsets, tile_width)
        return lax.dynamic_update_slice(
            result, band_cross, (jnp.int32(0), jnp.int32(0), jnp.int32(0), bin_start)
        )

    result = jnp.zeros((tile_width, offsets.shape[0], 2, bins), jnp.float32)
    return lax.fori_loop(0, bins // BAND, one_band, result)


def solution(mesh):
    return jax.shard_map(
        per_device,
        mesh=mesh,
        in_specs=(P("tm", "groups"), P(("groups", "tm")), P("groups"), P("groups", None), P()),
        out_specs=P(("groups", "tm"), None, None, None),
        check_vma=False,
    )
```

profile of v0, /device:TPU:10, one launch (start us, length us, event | category | flops | bytes accessed | tf_op | source)
XLA Modules:
  0.0 279.5 jit_solution(15077811135383140968)
XLA Ops:
  0.0 3.3 %copy.13 = bf16[256,4096]{0,1:T(8,128)(2,1)S(1)} copy(bf16[256,4096]{1,0:T(8,128)(2,1)} %param.7) | data formatting | bytes 4194304 | tf_op args[0]
  3.3 1.5 broadcast_multiply_fusion
  4.8 2.0 fusion.44
  7.5 30.6 %all_to_all.30 = bf16[256,16,128]{0,2,1:T(8,128)(2,1)S(1)} all-to-all(bf16[256,16,128]{0,2,1:T(8,128)(2,1)S(1)} %fusion.41), channel_id=1, replica_groups=mesh['groups'=2,'tm'=16] {'tm'}, dimensions={1} | all-to-all | bytes 2097152 | tf_op jit(solution)/shard_map/all_to_all | solution.py:102
  38.1 5.2 %all-to-all-start.1 = ((bf16[256,16,256]{0,2,1:T(8,128)(2,1)}), bf16[256,16,256]{0,2,1:T(8,128)(2,1)S(1)}, u32[]{:S(2)}, u32[]{:S(2)}) async-start(bf16[256,16,256]{0,2,1:T(8,128)(2,1)} %bitcast.5), calls=%async_computation.1 | async-start | bytes 4194304 | tf_op jit(solution)/shard_map/all_to_all | solution.py:101
  56.4 34.0 %all-to-all-done.1 = bf16[256,16,256]{0,2,1:T(8,128)(2,1)S(1)} async-done(((bf16[256,16,256]{0,2,1:T(8,128)(2,1)}), bf16[256,16,256]{0,2,1:T(8,128)(2,1)S(1)}, u32[]{:S(2)}, u32[]{:S(2)}) %all-to-all-start.1) | async-done | bytes 2097184 | tf_op jit(solution)/shard_map/all_to_all | solution.py:101
  90.4 2.4 copy.15
  93.3 185.2 %while.19 = (s32[]{:T(128)}, f32[16,4,2,2048]{3,2,1,0:T(2,128)S(1)}, bf16[4096,128]{1,0:T(8,128)(2,1)}, f32[16,8]{1,0:T(8,128)}, bf16[4096,256]{1,0:T(8,128)(2,1...) while((s32[]{:T(128)}, ...), condition=%wide.wide.region_14.15_spmd.clone.clone, body=%wide.wide.region_1.14_spmd.clone.clone.sunk | while | flops 1649076224 | bytes 42145152 | solution.py:130
  93.6 17.5 %multiply_subtract_fusion.3 = (f32[4096,256]{1,0:T(8,128)S(1)}, f32[4096,256]{1,0:T(8,128)S(1)}) fusion(f32[4096]{0:T(1024)S(1)} %get-tuple-element.806, f32[4096]{0:T(1024)S(1)} %get-tuple-element.807), kind=kLoop, calls=%fused_computation.13.clone.clone.1 | loop fusion | flops 22020096 | bytes 8421376 | tf_op jit(solution)/shard_map/while/body/eval_jaxpr/sub | solution.py:27
  111.1 2.2 fusion.71
  116.7 17.5 %multiply_subtract_fusion.3 = (f32[4096,256]{1,0:T(8,128)S(1)}, f32[4096,256]{1,0:T(8,128)S(1)}) fusion(f32[4096]{0:T(1024)S(1)} %get-tuple-element.806, f32[4096]{0:T(1024)S(1)} %get-tuple-element.807), kind=kLoop, calls=%fused_computation.13.clone.clone.1 | loop fusion | flops 22020096 | bytes 8421376 | tf_op jit(solution)/shard_map/while/body/eval_jaxpr/sub | solution.py:27
  134.3 2.2 fusion.71
  139.8 17.5 %multiply_subtract_fusion.3 = (f32[4096,256]{1,0:T(8,128)S(1)}, f32[4096,256]{1,0:T(8,128)S(1)}) fusion(f32[4096]{0:T(1024)S(1)} %get-tuple-element.806, f32[4096]{0:T(1024)S(1)} %get-tuple-element.807), kind=kLoop, calls=%fused_computation.13.clone.clone.1 | loop fusion | flops 22020096 | bytes 8421376 | tf_op jit(solution)/shard_map/while/body/eval_jaxpr/sub | solution.py:27
  157.4 2.2 fusion.71
  163.0 17.5 %multiply_subtract_fusion.3 = (f32[4096,256]{1,0:T(8,128)S(1)}, f32[4096,256]{1,0:T(8,128)S(1)}) fusion(f32[4096]{0:T(1024)S(1)} %get-tuple-element.806, f32[4096]{0:T(1024)S(1)} %get-tuple-element.807), kind=kLoop, calls=%fused_computation.13.clone.clone.1 | loop fusion | flops 22020096 | bytes 8421376 | tf_op jit(solution)/shard_map/while/body/eval_jaxpr/sub | solution.py:27
  180.5 2.2 fusion.71
  186.1 17.5 %multiply_subtract_fusion.3 = (f32[4096,256]{1,0:T(8,128)S(1)}, f32[4096,256]{1,0:T(8,128)S(1)}) fusion(f32[4096]{0:T(1024)S(1)} %get-tuple-element.806, f32[4096]{0:T(1024)S(1)} %get-tuple-element.807), kind=kLoop, calls=%fused_computation.13.clone.clone.1 | loop fusion | flops 22020096 | bytes 8421376 | tf_op jit(solution)/shard_map/while/body/eval_jaxpr/sub | solution.py:27
  203.6 2.2 fusion.71
  209.2 17.5 %multiply_subtract_fusion.3 = (f32[4096,256]{1,0:T(8,128)S(1)}, f32[4096,256]{1,0:T(8,128)S(1)}) fusion(f32[4096]{0:T(1024)S(1)} %get-tuple-element.806, f32[4096]{0:T(1024)S(1)} %get-tuple-element.807), kind=kLoop, calls=%fused_computation.13.clone.clone.1 | loop fusion | flops 22020096 | bytes 8421376 | tf_op jit(solution)/shard_map/while/body/eval_jaxpr/sub | solution.py:27
  226.8 2.2 fusion.71
  232.3 17.5 %multiply_subtract_fusion.3 = (f32[4096,256]{1,0:T(8,128)S(1)}, f32[4096,256]{1,0:T(8,128)S(1)}) fusion(f32[4096]{0:T(1024)S(1)} %get-tuple-element.806, f32[4096]{0:T(1024)S(1)} %get-tuple-element.807), kind=kLoop, calls=%fused_computation.13.clone.clone.1 | loop fusion | flops 22020096 | bytes 8421376 | tf_op jit(solution)/shard_map/while/body/eval_jaxpr/sub | solution.py:27
  249.9 2.2 fusion.71
  255.5 17.5 %multiply_subtract_fusion.3 = (f32[4096,256]{1,0:T(8,128)S(1)}, f32[4096,256]{1,0:T(8,128)S(1)}) fusion(f32[4096]{0:T(1024)S(1)} %get-tuple-element.806, f32[4096]{0:T(1024)S(1)} %get-tuple-element.807), kind=kLoop, calls=%fused_computation.13.clone.clone.1 | loop fusion | flops 22020096 | bytes 8421376 | tf_op jit(solution)/shard_map/while/body/eval_jaxpr/sub | solution.py:27
  273.0 2.2 fusion.71
  (225 shorter events, 30.8 us)
Async XLA Ops:
  0.0 3.3 %copy-start.6 = (s32[256]{0:T(256)S(1)}, s32[256]{0:T(256)}, u32[]{:S(2)}) copy-start(s32[256]{0:T(256)} %param.8) | copy-start | bytes 3076
  6.8 36.4 %copy-start.5 = (s32[4,2]{0,1:T(2,128)S(1)}, s32[4,2]{0,1:T(2,128)}, u32[]{:S(2)}) copy-start(s32[4,2]{0,1:T(2,128)} %param.11) | copy-start | bytes 100
  6.8 47.0 %copy-start.7 = (s32[16]{0:T(128)S(1)}, s32[16]{0:T(128)}, u32[]{:S(2)}) copy-start(s32[16]{0:T(128)} %param.9) | copy-start | bytes 196
  6.8 47.1 %copy-start.4 = (s32[16,256]{1,0:T(8,128)S(1)}, s32[16,256]{1,0:T(8,128)}, u32[]{:S(2)}) copy-start(s32[16,256]{1,0:T(8,128)} %param.10) | copy-start | bytes 49156
  38.1 52.3 %all-to-all-start.1 = ((bf16[256,16,256]{0,2,1:T(8,128)(2,1)}), bf16[256,16,256]{0,2,1:T(8,128)(2,1)S(1)}, u32[]{:S(2)}, u32[]{:S(2)}) async-start(bf16[256,16,256]{0,2,1:T(8,128)(2,1)} %bitcast.5), calls=%async_computation.1 | async-start | bytes 4194304 | tf_op jit(solution)/shard_map/all_to_all | solution.py:101
  54.8 38.5 %copy-start.2 = (f32[16,8]{1,0:T(8,128)}, f32[16,8]{1,0:T(8,128)S(1)}, u32[]{:S(2)}) copy-start(f32[16,8]{1,0:T(8,128)S(1)} %pad_maximum_fusion) | copy-start | bytes 1540
  55.0 38.3 %copy-start.3 = (f32[1,16,16]{2,1,0:T(8,128)}, f32[1,16,16]{2,1,0:T(8,128)S(1)}, u32[]{:S(2)}) copy-start(f32[1,16,16]{2,1,0:T(8,128)S(1)} %slice.243) | copy-start | bytes 3076
  111.1 2.3 copy-start
  134.2 2.3 copy-start
  157.4 2.3 copy-start
  180.5 2.3 copy-start
  203.6 2.3 copy-start
  226.8 2.3 copy-start
  249.9 2.3 copy-start
  273.0 2.3 copy-start
  278.5 1.0 copy-start.1
where the time goes:
time: 280 us; the launch traced here: 279 us
  other arithmetic  157 us (56%)
  waiting for transfers between devices  34 us (12%)
  blocking collectives  30.6 us (11%)
  matrix products  28.3 us (10%)
  local copies, waits for them, and re-layouts  13 us (5%)
  between operations  10.1 us (4%)
  starting transfers between devices  5.19 us (2%)
    sub x8, other arithmetic, rotated_table(): real_part = base_cos * phase_cos - base_sin * phase_sin  140 us
    all_to_all x1, waiting for transfers between devices, per_device(): lax.all_to_all(grouped, 'tm', split_axis=1, concat_axis=0, tiled=True)  34 us
    all_to_all x1, blocking collectives, per_device(): lax.all_to_all(margins, 'tm', split_axis=1, concat_axis=0, tiled=True)  30.6 us
    dot_general x16, matrix products, transform(): lax.dot_general(columns, table, (((0,), (0,)), ((), ())), preferred_eleme...  28.3 us
  transfers between devices with their start and end apart: 1, of which 1 were waited for; matrix products, arithmetic and copies ran while one was open for 1% of the time, Pallas kernels for 0%

commit v1 on v0

v1 whole, which is shorter than its diff:
```python
import functools
import math

import jax
import jax.numpy as jnp
import numpy as np
from jax import lax
from jax.experimental import pallas as pl
from jax.experimental.pallas import tpu as pltpu
from jax.sharding import PartitionSpec as P

ROWS = 16
REACH = 4
RADIX = 16
LANES = 128


def dft_tables(frames_len):
    inner = frames_len // RADIX
    steps = np.arange(inner)
    angles = 2.0 * np.pi * (np.outer(steps, steps) % inner) / inner
    table = np.concatenate([np.cos(angles), -np.sin(angles)], axis=1) / math.sqrt(frames_len)
    turns = 2.0 * np.pi * np.outer(np.arange(RADIX), steps) / frames_len
    twiddle = np.stack([np.cos(turns), -np.sin(turns)], axis=1)
    twiddle = np.broadcast_to(twiddle[:, :, None, :], (RADIX, 2, 8, inner))
    return jnp.asarray(table, jnp.bfloat16), jnp.asarray(twiddle, jnp.float32)


def compact_kernel(count_ref, valid_ref, map_ref, frames_ref, out_ref):
    step = pl.program_id(0)
    batch, frame_dev, slots = out_ref.shape
    tile_pix = frames_ref.shape[1] // batch
    per_phase = frame_dev // RADIX
    row = lax.broadcasted_iota(jnp.int32, (frame_dev, frame_dev), 0)
    col = lax.broadcasted_iota(jnp.int32, (frame_dev, frame_dev), 1)
    source = row % per_phase * RADIX + row // per_phase
    keep = jnp.broadcast_to(valid_ref[...], (frame_dev, frame_dev))
    order = jnp.where(col == source, keep, 0).astype(jnp.float32).astype(jnp.bfloat16)
    pixel = lax.broadcasted_iota(jnp.int32, (tile_pix, slots), 0)
    slot = lax.broadcasted_iota(jnp.int32, (tile_pix, slots), 1)
    for pair in range(batch // 2):
        parts = []
        for which in (2 * pair, 2 * pair + 1):
            count = count_ref[step * batch + which]
            held = jnp.broadcast_to(map_ref[0, which : which + 1, :slots], (tile_pix, slots))
            hot = jnp.where((held == pixel) & (slot < count), 1.0, 0.0).astype(jnp.bfloat16)
            block = frames_ref[:, which * tile_pix : (which + 1) * tile_pix]
            parts.append(jnp.dot(block, hot, preferred_element_type=jnp.float32))
        both = jnp.concatenate(parts, axis=1).astype(jnp.bfloat16)
        both = jnp.dot(order, both, preferred_element_type=jnp.float32).astype(jnp.bfloat16)
        out_ref[2 * pair] = both[:, :slots]
        out_ref[2 * pair + 1] = both[:, slots:]


def compact(frames, frame_valid, valid_count, block_map):
    frame_dev, pixel_count = frames.shape
    tile_count, tile_pix = block_map.shape
    slots = tile_pix // 2
    batch = 4
    return pl.pallas_call(
        compact_kernel,
        name="compact",
        grid=(tile_count // batch,),
        out_shape=jax.ShapeDtypeStruct((tile_count, frame_dev, slots), jnp.bfloat16),
        in_specs=[
            pl.BlockSpec(memory_space=pltpu.SMEM),
            pl.BlockSpec((1, frame_dev), lambda i: (0, 0)),
            pl.BlockSpec((1, batch, tile_pix), lambda i: (i, 0, 0)),
            pl.BlockSpec((frame_dev, batch * tile_pix), lambda i: (0, i)),
        ],
        out_specs=pl.BlockSpec((batch, frame_dev, slots), lambda i: (i, 0, 0)),
    )(
        valid_count,
        frame_valid.reshape(1, frame_dev),
        block_map.reshape(tile_count // batch, batch, tile_pix),
        frames,
    )


def rotate(real, imag, cos, sin):
    return real * cos - imag * sin, real * sin + imag * cos


def four_point(values):
    (r0, i0), (r1, i1), (r2, i2), (r3, i3) = values
    er, ei, fr, fi = r0 + r2, i0 + i2, r0 - r2, i0 - i2
    gr, gi, hr, hi = r1 + r3, i1 + i3, r1 - r3, i1 - i3
    return [(er + gr, ei + gi), (fr + hi, fi - hr), (er - gr, ei - gi), (fr - hi, fi + hr)]


def sixteen_point_low(values):
    inner = [four_point([values[4 * n + m] for n in range(4)]) for m in range(4)]
    low = [None] * 8
    for k in range(4):
        parts = []
        for m in range(4):
            real, imag = inner[m][k]
            turn = m * k % 16
            if turn == 0:
                parts.append((real, imag))
            elif turn == 4:
                parts.append((imag, -real))
            else:
                angle = -2.0 * math.pi * turn / 16
                parts.append(rotate(real, imag, math.cos(angle), math.sin(angle)))
        (r0, i0), (r1, i1), (r2, i2), (r3, i3) = parts
        low[k] = ((r0 + r2) + (r1 + r3), (i0 + i2) + (i1 + i3))
        low[k + 4] = ((r0 - r2) + (i1 - i3), (i0 - i2) - (r1 - r3))
    return low


def transform_kernel(place_ref, frames_ref, table_ref, twiddle_ref, own_ref, left_ref, right_ref, phases, spread):
    slots = own_ref.shape[0]
    rows = own_ref.shape[1]
    half = rows // 2
    inner = table_ref.shape[0]
    width = place_ref.shape[0] // (ROWS + 2 * REACH)
    for phase in range(RADIX):
        if len(frames_ref.shape) == 3:
            per_phase = frames_ref.shape[1] // RADIX
            block = frames_ref[:, phase * per_phase : (phase + 1) * per_phase, :].reshape(inner, slots)
        else:
            block = frames_ref[phase].reshape(inner, slots)
        phases[phase] = lax.dot_general(
            block, table_ref[...], (((0,), (0,)), ((), ())), preferred_element_type=jnp.float32
        )
    chunks = inner // LANES

    def one_group(group, carry):
        first = pl.multiple_of(group * 8, 8)
        for chunk in range(chunks):
            lanes = pl.ds(chunk * LANES, LANES)
            values = []
            for phase in range(RADIX):
                real = phases[phase, pl.ds(first, 8), lanes]
                imag = phases[phase, pl.ds(first, 8), pl.ds(inner + chunk * LANES, LANES)]
                if phase > 0:
                    real, imag = rotate(real, imag, twiddle_ref[phase, 0, :, lanes], twiddle_ref[phase, 1, :, lanes])
                values.append((real, imag))
            for high, (real, imag) in enumerate(sixteen_point_low(values)):
                at = first * rows + high * chunks + chunk
                spread[pl.ds(at, 8, stride=rows), :] = real
                spread[pl.ds(at + half, 8, stride=rows), :] = imag
        return carry

    lax.fori_loop(0, slots // 8, one_group, 0)

    def one_slot(slot, carry):
        at = pl.multiple_of(slot * rows, rows)
        own_ref[slot] = spread[pl.ds(at, rows), :].astype(jnp.bfloat16)
        return carry

    lax.fori_loop(0, slots, one_slot, 0, unroll=4)
    spread[pl.ds(slots * rows, rows), :] = jnp.zeros((rows, LANES), jnp.float32)

    def one_edge(spot, carry):
        row = spot // REACH
        column = spot % REACH
        base = (row + REACH) * width + REACH + column
        slot = jnp.minimum(place_ref[base], slots)
        left_ref[spot] = spread[pl.ds(pl.multiple_of(slot * rows, rows), rows), :].astype(jnp.bfloat16)
        slot = jnp.minimum(place_ref[base + width - 3 * REACH], slots)
        right_ref[spot] = spread[pl.ds(pl.multiple_of(slot * rows, rows), rows), :].astype(jnp.bfloat16)
        return carry

    lax.fori_loop(0, ROWS * REACH, one_edge, 0, unroll=4)


def transform(place, tile_frames, slots, frames_len):
    table, twiddle = dft_tables(frames_len)
    inner = frames_len // RADIX
    rows = frames_len // LANES
    edge = ROWS * REACH
    whole = pl.BlockSpec(memory_space=pltpu.VMEM)
    return pl.pallas_call(
        transform_kernel,
        name="transform",
        out_shape=(
            jax.ShapeDtypeStruct((slots, rows, LANES), jnp.bfloat16),
            jax.ShapeDtypeStruct((edge, rows, LANES), jnp.bfloat16),
            jax.ShapeDtypeStruct((edge, rows, LANES), jnp.bfloat16),
        ),
        in_specs=[pl.BlockSpec(memory_space=pltpu.SMEM), whole, whole, whole],
        out_specs=(whole, whole, whole),
        scratch_shapes=[
            pltpu.VMEM((RADIX, slots, 2 * inner), jnp.float32),
            pltpu.VMEM(((slots + 1) * rows, LANES), jnp.float32),
        ],
    )(place, tile_frames, table, twiddle)


def cross_kernel(place_ref, offset_ref, map_ref, count_ref, own_hbm, right_hbm, left_hbm, out_ref, held, total, pairs, sem):
    slots, rows, _ = own_hbm.shape
    half = rows // 2
    edge = ROWS * REACH
    width = place_ref.shape[0] // (ROWS + 2 * REACH)
    tile_width = width - 2 * REACH
    empty = slots + 2 * edge
    copies = [
        pltpu.make_async_copy(own_hbm, held.at[pl.ds(0, slots)], sem.at[0]),
        pltpu.make_async_copy(right_hbm, held.at[pl.ds(slots, edge)], sem.at[1]),
        pltpu.make_async_copy(left_hbm, held.at[pl.ds(slots + edge, edge)], sem.at[2]),
    ]
    for copy in copies:
        copy.start()
    columns = total.shape[0]
    held[empty] = jnp.zeros((rows, LANES), jnp.bfloat16)

    def clear(spot, carry):
        total[spot] = jnp.zeros((rows, LANES), jnp.float32)
        pairs[spot] = 0
        return carry

    lax.fori_loop(0, columns, clear, 0)
    for copy in copies:
        copy.wait()
    offsets = offset_ref.shape[0]
    shifts = [offset_ref[j, 0] * width + offset_ref[j, 1] for j in range(offsets)]

    def one_slot(slot, carry):
        pixel = map_ref[slot]
        row = pixel // tile_width
        column = pixel % tile_width
        base = (row + REACH) * width + REACH + column
        own_real = held[slot, :half].astype(jnp.float32)
        own_imag = held[slot, half:].astype(jnp.float32)
        for j in range(offsets):
            other = place_ref[base + shifts[j]]
            at = column * offsets + j
            pairs[at] = pairs[at] + jnp.where(other < empty, 1, 0)
            real = held[other, :half].astype(jnp.float32)
            imag = held[other, half:].astype(jnp.float32)
            total[at, :half] += own_real * real + own_imag * imag
            total[at, half:] += own_imag * real - own_real * imag
        return carry

    lax.fori_loop(0, count_ref[0], one_slot, 0)

    def finish(spot, carry):
        seen = jnp.full((1, LANES), pairs[spot], jnp.int32).astype(jnp.float32)
        scaling = 1.0 / jnp.maximum(seen, 1.0)
        out_ref[spot, pl.ds(0, half, stride=2), :] = total[spot, :half] * scaling
        out_ref[spot, pl.ds(1, half, stride=2), :] = total[spot, half:] * scaling
        return carry

    lax.fori_loop(0, columns, finish, 0)


def cross(place, offsets, own_map, own_count, own, from_right, from_left, tile_width):
    slots, rows, _ = own.shape
    spots = tile_width * offsets.shape[0]
    small = pl.BlockSpec(memory_space=pltpu.SMEM)
    large = pl.BlockSpec(memory_space=pl.ANY)
    return pl.pallas_call(
        cross_kernel,
        name="cross",
        out_shape=jax.ShapeDtypeStruct((spots, rows, LANES), jnp.float32),
        in_specs=[small, small, small, small, large, large, large],
        out_specs=pl.BlockSpec(memory_space=pltpu.VMEM),
        scratch_shapes=[
            pltpu.VMEM((slots + 2 * ROWS * REACH + 1, rows, LANES), jnp.bfloat16),
            pltpu.VMEM((spots, rows, LANES), jnp.float32),
            pltpu.SMEM((spots,), jnp.int32),
            pltpu.SemaphoreType.DMA((3,)),
        ],
    )(place, offsets, own_map, own_count, own, from_right, from_left)


def neighbour_places(valid_count, block_map, position):
    tile_pix = block_map.shape[1]
    slots = tile_pix // 2
    tile_width = tile_pix // ROWS
    edge = ROWS * REACH
    empty = slots + 2 * edge
    padded_count = jnp.pad(valid_count, ((1, 1),))
    padded_map = jnp.pad(block_map, ((1, 1), (0, 0)))
    counts = lax.dynamic_slice_in_dim(padded_count, position, 3, 0)
    maps = lax.dynamic_slice_in_dim(padded_map, position, 3, 0)[:, :slots]
    slot_idx = jnp.arange(slots, dtype=jnp.int32)
    pixel_idx = jnp.arange(tile_pix, dtype=jnp.int32)
    match = (maps[:, :, None] == pixel_idx[None, None, :]) & (slot_idx[None, :, None] < counts[:, None, None])
    found = jnp.max(jnp.where(match, slot_idx[None, :, None], -1), axis=1)
    grid = found.reshape(3, ROWS, tile_width)
    spot = (jnp.arange(ROWS, dtype=jnp.int32) * REACH)[:, None] + jnp.arange(REACH, dtype=jnp.int32)[None, :]
    own = jnp.where(grid[1] >= 0, grid[1], empty)
    right = jnp.where(grid[2][:, :REACH] >= 0, slots + spot, empty)
    left = jnp.where(grid[0][:, tile_width - REACH :] >= 0, slots + edge + spot, empty)
    place = jnp.concatenate([left, own, right], axis=1)
    place = jnp.pad(place, ((REACH, REACH), (0, 0)), constant_values=empty)
    return place.reshape(-1), maps[1], counts[1:2]


def per_device(frames, frame_valid, valid_count, block_map, offsets):
    devices = lax.axis_size("tm")
    position = lax.axis_index("tm")
    frame_dev = frames.shape[0]
    frames_len = frame_dev * devices
    tile_pix = block_map.shape[1]
    slots = tile_pix // 2
    sent = compact(frames, frame_valid, valid_count, block_map)
    tile_frames = lax.all_to_all(sent, "tm", split_axis=0, concat_axis=0, tiled=True)
    if frame_dev // RADIX % 16 != 0:
        tile_frames = tile_frames.reshape(devices, RADIX, frame_dev // RADIX, slots)
        tile_frames = tile_frames.transpose(1, 0, 2, 3).reshape(RADIX, frames_len // RADIX, slots)
    place, own_map, own_count = neighbour_places(valid_count, block_map, position)
    own, left, right = transform(place, tile_frames, slots, frames_len)
    from_right = lax.ppermute(left, "tm", [(i, i - 1) for i in range(1, devices)])
    from_left = lax.ppermute(right, "tm", [(i, i + 1) for i in range(devices - 1)])
    tile_width = tile_pix // ROWS
    result = cross(place, offsets, own_map, own_count, own, from_right, from_left, tile_width)
    bins = frames_len // 2
    result = result.reshape(tile_width, offsets.shape[0], bins // LANES, 2, LANES)
    return result.transpose(0, 1, 3, 2, 4).reshape(tile_width, offsets.shape[0], 2, bins)


def solution(mesh):
    return jax.shard_map(
        per_device,
        mesh=mesh,
        in_specs=(P("tm", "groups"), P(("groups", "tm")), P("groups"), P("groups", None), P()),
        out_specs=P(("groups", "tm"), None, None, None),
        check_vma=False,
    )
```

time: 280 us -> 72.2 us (0.26)
  other arithmetic: 157 us -> 0.43 us
  blocking collectives: 30.6 us -> 0 us
  matrix products: 28.3 us -> 0 us
  Pallas kernels: 0 us -> 19.1 us
  between operations: 10.1 us -> 0.05 us
  local copies, waits for them, and re-layouts: 13 us -> 5.98 us
  starting transfers between devices: 5.19 us -> 10.8 us
    sub x8 -> x0, other arithmetic: 140 us -> none  [rotated_table(): real_part = base_cos * phase_cos - base_sin * phase_sin]
    all_to_all x1 -> x0, blocking collectives: 30.6 us -> none  [per_device(): lax.all_to_all(margins, 'tm', split_axis=1, concat_axis=0, tiled=True)]
    dot_general x16 -> x0, matrix products: 28.3 us -> none  [transform(): lax.dot_general(columns, table, (((0,), (0,)), ((), ())), preferred_eleme...]
    pallas_call x0 -> x3, Pallas kernels: none -> 19.1 us  [the longest x1 7.47 us: cross(): pl.pallas_call(cross_kernel, name='cross', out_shape=jax.ShapeDtypeStruct...]
    ppermute x0 -> x2, waiting for transfers between devices: none -> 11.5 us  [the longest x1 8.84 us: per_device(): lax.ppermute(left, 'tm', [(i, i - 1) for i in range(1, devices)])]
    all_to_all x1, waiting for transfers between devices: 34 us -> 23.1 us  [per_device(): lax.all_to_all(sent, 'tm', split_axis=0, concat_axis=0, tiled=True)]
    reduce_sum x25 -> x0, other arithmetic: 8.7 us -> none  [the longest x8 3.68 us: cross_block(): imag_part = jnp.sum(own_imag * other_real - own_real * other_imag, axis=0)]
    ppermute x0 -> x2, starting transfers between devices: none -> 4.44 us  [the longest x1 2.52 us: per_device(): lax.ppermute(left, 'tm', [(i, i - 1) for i in range(1, devices)])]
  transfers between devices with their start and end apart: 1 -> 3, of which waited for: 1 -> 3; matrix products, arithmetic and copies ran while one was open for 1% -> 5% of each run, Pallas kernels for 0% -> 0%
where the time goes in v1:
time: 72.2 us; the launch traced here: 71 us
  waiting for transfers between devices  34.6 us (48%)
  Pallas kernels  19.1 us (26%)
  starting transfers between devices  10.8 us (15%)
  local copies, waits for them, and re-layouts  5.98 us (8%)
    all_to_all x1, waiting for transfers between devices, per_device(): lax.all_to_all(sent, 'tm', split_axis=0, concat_axis=0, tiled=True)  23.1 us
    ppermute x1, waiting for transfers between devices, per_device(): lax.ppermute(left, 'tm', [(i, i - 1) for i in range(1, devices)])  8.84 us
    pallas_call x1, Pallas kernels, cross(): pl.pallas_call(cross_kernel, name='cross', out_shape=jax.ShapeDtypeStruct...  7.47 us
    pallas_call x1, Pallas kernels, transform(): pl.pallas_call(transform_kernel, name='transform', out_shape=(jax.ShapeDt...  6.63 us
    all_to_all x1, starting transfers between devices, per_device(): lax.all_to_all(sent, 'tm', split_axis=0, concat_axis=0, tiled=True)  6.37 us
    pallas_call x1, Pallas kernels, compact(): pl.pallas_call(compact_kernel, name='compact', grid=(tile_count // batch,...  5.04 us
    ppermute x1, waiting for transfers between devices, per_device(): lax.ppermute(right, 'tm', [(i, i + 1) for i in range(devices - 1)])  2.65 us
    ppermute x1, starting transfers between devices, per_device(): lax.ppermute(left, 'tm', [(i, i - 1) for i in range(1, devices)])  2.52 us
  transfers between devices with their start and end apart: 3, of which 3 were waited for; matrix products, arithmetic and copies ran while one was open for 5% of the time, Pallas kernels for 0%

profile of v1, /device:TPU:10, one launch (start us, length us, event | category | flops | bytes accessed | tf_op | source)
XLA Modules:
  0.0 71.0 jit_solution(270326521525093975)
XLA Ops:
  0.0 1.3 %reshape.54.map_ref = s32[4,4,256]{2,1,0:T(4,128)} reshape(s32[16,256]{1,0:T(8,128)} %param.10) | data formatting | bytes 32768 | tf_op jit(solution)/shard_map/reshape | solution.py:75
  1.3 5.0 %compact.1 = bf16[16,256,128]{2,1,0:T(8,128)(2,1)} custom-call(s32[16]{0:T(128)} %count_ref.1, s32[1,256]{1,0:T(1,128)} %bitcast.8, s32[4,4,256]{2,1,0:T(4,128)} %reshape.54.map_ref, bf16[256,4096]{1,0:T(8,128)(2,1)} %frames_ref.1), custom_call_target="tpu_custom_call" | custom-call | tf_op jit(solution)/shard_map/compact/pallas_call | solution.py:60
  6.4 6.4 %all-to-all-start = ((bf16[16,256,128]{2,1,0:T(8,128)(2,1)}), bf16[16,256,128]{2,1,0:T(8,128)(2,1)S(1)}, u32[]{:S(2)}, u32[]{:S(2)}) async-start(bf16[16,256,128]{2,1,0:T(8,128)(2,1)} %compact.1), calls=%async_computation | async-start | bytes 2097152 | tf_op jit(solution)/shard_map/all_to_all | solution.py:301
  12.7 0.1 pad_dynamic-slice_fusion.2
  12.8 0.1 iota_compare_fusion.1
  12.9 0.2 select_reduce_fusion
  13.1 0.1 squeeze.13
  13.2 0.1 squeeze.15
  13.3 0.1 squeeze.14
  13.4 0.1 add_select_fusion.1
  13.5 0.1 pad_add_fusion
  13.6 0.7 reshape.52.place_ref
  14.2 23.1 %all-to-all-done.frames_ref = bf16[16,256,128]{2,1,0:T(8,128)(2,1)S(1)} async-done(((bf16[16,256,128]{2,1,0:T(8,128)(2,1)}), bf16[16,256,128]{2,1,0:T(8,128)(2,1)S(1)}, u32[]{:S(2)}, u32[]{:S(2)}) %all-to-all-start) | async-done | bytes 1048608 | tf_op jit(solution)/shard_map/all_to_all | solution.py:301
  37.3 1.0 %copy-done = bf16[16,256,128]{2,1,0:T(8,128)(2,1)} copy-done((bf16[16,256,128]{2,1,0:T(8,128)(2,1)}, bf16[16,256,128]{2,1,0:T(8,128)(2,1)S(1)}, u32[]{:S(2)}) %copy-start) | copy-done | bytes 1048600
  38.3 6.6 %transform.1 = (bf16[128,32,128]{2,1,0:T(8,128)(2,1)}, bf16[64,32,128]{2,1,0:T(8,128)(2,1)}, bf16[64,32,128]{2,1,0:T(8,128)(2,1)}) custom-call(s32[576]{0:T(1024)} %reshape.52.place_ref, bf16[16,256,128]{2,1,0:T(8,128)(2,1)} %copy-done, bf16[256,512]{1,0:T(8,128)(2,1)} %constant.9.clone.table_ref, f32[16,2,8,256]{3,2,1,0:T(8,128)} %constant.10.clone.twiddle_ref), custom_call_target="tpu_custom_call" | custom-call | tf_op jit(solution)/shard_map/transform/pallas_call | solution.py:175
  44.9 2.5 %collective-permute-start = (bf16[64,32,128]{2,1,0:T(8,128)(2,1)}, bf16[64,32,128]{2,1,0:T(8,128)(2,1)S(1)}, u32[]{:S(2)}, u32[]{:S(2)}) collective-permute-start(bf16[64,32,128]{2,1,0:T(8,128)(2,1)} %get-tuple-element.9), channel_id=1, source_target_pairs={{1,0},{2,1},{3,2},{4,3},{5,4},{6,5},{7,6},{8,7},{9,8},{10,9},{11,1... | collective-permute-start | bytes 1572872 | tf_op jit(solution)/shard_map/ppermute | solution.py:307
  47.4 1.9 %collective-permute-start.1 = (bf16[64,32,128]{2,1,0:T(8,128)(2,1)}, bf16[64,32,128]{2,1,0:T(8,128)(2,1)S(1)}, u32[]{:S(2)}, u32[]{:S(2)}) collective-permute-start(bf16[64,32,128]{2,1,0:T(8,128)(2,1)} %get-tuple-element.10), channel_id=1, source_target_pairs={{0,1},{1,2},{2,3},{3,4},{4,5},{5,6},{6,7},{7,8},{8,9},{9,10},{10,1... | collective-permute-start | bytes 1572872 | tf_op jit(solution)/shard_map/ppermute | solution.py:308
  49.4 0.6 slice.36.count_ref
  50.0 0.7 copy.10.offset_ref
  50.6 0.6 fusion.1.map_ref
  51.2 8.8 %collective-permute-done.right_hbm = bf16[64,32,128]{2,1,0:T(8,128)(2,1)S(1)} collective-permute-done((bf16[64,32,128]{2,1,0:T(8,128)(2,1)}, bf16[64,32,128]{2,1,0:T(8,128)(2,1)S(1)}, u32[]{:S(2)}, u32[]{:S(2)}) %collective-permute-start) | collective-permute-done | bytes 524320 | tf_op jit(solution)/shard_map/ppermute | solution.py:307
  60.1 2.6 %collective-permute-done.1.left_hbm = bf16[64,32,128]{2,1,0:T(8,128)(2,1)S(1)} collective-permute-done((bf16[64,32,128]{2,1,0:T(8,128)(2,1)}, bf16[64,32,128]{2,1,0:T(8,128)(2,1)S(1)}, u32[]{:S(2)}, u32[]{:S(2)}) %collective-permute-start.1) | collective-permute-done | bytes 524320 | tf_op jit(solution)/shard_map/ppermute | solution.py:308
  62.7 0.8 %copy-done.2 = bf16[64,32,128]{2,1,0:T(8,128)(2,1)} copy-done((bf16[64,32,128]{2,1,0:T(8,128)(2,1)}, bf16[64,32,128]{2,1,0:T(8,128)(2,1)S(1)}, u32[]{:S(2)}) %copy-start.2) | copy-done | bytes 524312
  63.5 7.5 %cross.1 = f32[64,32,128]{2,1,0:T(8,128)} custom-call(s32[576]{0:T(1024)} %reshape.52.place_ref, s32[4,2]{1,0:T(4,128)} %copy.10.offset_ref, s32[128]{0:T(128)} %fusion.1.map_ref, s32[1]{0:T(128)} %slice.36.count_ref, bf16[128,32,128]{2,1,0:T(8,128)(2,1)} %get-tuple-element.8.own_hbm, bf16[64,32,128]{2,1,0:T(8,128)(2,1)} %copy-done.1, ...), custom_call_target="tpu_custom_call" | custom-call | tf_op jit(solution)/shard_map/cross/pallas_call | solution.py:254
  (15 shorter events, 0.1 us)
Async XLA Ops:
  1.3 11.4 %copy-start.5 = (s32[16]{0:T(128)S(1)}, s32[16]{0:T(128)}, u32[]{:S(2)}) copy-start(s32[16]{0:T(128)} %count_ref.1) | copy-start | bytes 196
  1.3 11.5 %copy-start.3 = (s32[16,256]{1,0:T(8,128)S(1)}, s32[16,256]{1,0:T(8,128)}, u32[]{:S(2)}) copy-start(s32[16,256]{1,0:T(8,128)} %param.10) | copy-start | bytes 49156
  6.4 43.6 %copy-start.4 = (s32[4,2]{0,1:T(2,128)S(1)}, s32[4,2]{0,1:T(2,128)}, u32[]{:S(2)}) copy-start(s32[4,2]{0,1:T(2,128)} %param.11) | copy-start | bytes 100
  6.4 30.9 %all-to-all-start = ((bf16[16,256,128]{2,1,0:T(8,128)(2,1)}), bf16[16,256,128]{2,1,0:T(8,128)(2,1)S(1)}, u32[]{:S(2)}, u32[]{:S(2)}) async-start(bf16[16,256,128]{2,1,0:T(8,128)(2,1)} %compact.1), calls=%async_computation | async-start | bytes 2097152 | tf_op jit(solution)/shard_map/all_to_all | solution.py:301
  37.3 1.0 %copy-start = (bf16[16,256,128]{2,1,0:T(8,128)(2,1)}, bf16[16,256,128]{2,1,0:T(8,128)(2,1)S(1)}, u32[]{:S(2)}) copy-start(bf16[16,256,128]{2,1,0:T(8,128)(2,1)S(1)} %all-to-all-done.frames_ref) | copy-start | bytes 3145732
  44.9 15.1 %collective-permute-start = (bf16[64,32,128]{2,1,0:T(8,128)(2,1)}, bf16[64,32,128]{2,1,0:T(8,128)(2,1)S(1)}, u32[]{:S(2)}, u32[]{:S(2)}) collective-permute-start(bf16[64,32,128]{2,1,0:T(8,128)(2,1)} %get-tuple-element.9), channel_id=1, source_target_pairs={{1,0},{2,1},{3,2},{4,3},{5,4},{6,5},{7,6},{8,7},{9,8},{10,9},{11,1... | collective-permute-start | bytes 1572872 | tf_op jit(solution)/shard_map/ppermute | solution.py:307
  47.4 15.3 %collective-permute-start.1 = (bf16[64,32,128]{2,1,0:T(8,128)(2,1)}, bf16[64,32,128]{2,1,0:T(8,128)(2,1)S(1)}, u32[]{:S(2)}, u32[]{:S(2)}) collective-permute-start(bf16[64,32,128]{2,1,0:T(8,128)(2,1)} %get-tuple-element.10), channel_id=1, source_target_pairs={{0,1},{1,2},{2,3},{3,4},{4,5},{5,6},{6,7},{7,8},{8,9},{9,10},{10,1... | collective-permute-start | bytes 1572872 | tf_op jit(solution)/shard_map/ppermute | solution.py:308
  60.1 2.7 %copy-start.1 = (bf16[64,32,128]{2,1,0:T(8,128)(2,1)}, bf16[64,32,128]{2,1,0:T(8,128)(2,1)S(1)}, u32[]{:S(2)}) copy-start(bf16[64,32,128]{2,1,0:T(8,128)(2,1)S(1)} %collective-permute-done.right_hbm) | copy-start | bytes 1572868
  62.7 0.8 %copy-start.2 = (bf16[64,32,128]{2,1,0:T(8,128)(2,1)}, bf16[64,32,128]{2,1,0:T(8,128)(2,1)S(1)}, u32[]{:S(2)}) copy-start(bf16[64,32,128]{2,1,0:T(8,128)(2,1)S(1)} %collective-permute-done.1.left_hbm) | copy-start | bytes 1572868

commit v2 on v1

v2 whole, which is shorter than its diff:
```python
import functools
import math

import jax
import jax.numpy as jnp
import numpy as np
from jax import lax
from jax.experimental import pallas as pl
from jax.experimental.pallas import tpu as pltpu
from jax.sharding import PartitionSpec as P

ROWS = 16
REACH = 4
RADIX = 16
LANES = 128
INFO = 10


def dft_tables(frames_len):
    inner = frames_len // RADIX
    steps = np.arange(inner)
    angles = 2.0 * np.pi * (np.outer(steps, steps) % inner) / inner
    table = np.concatenate([np.cos(angles), -np.sin(angles)], axis=1) / math.sqrt(frames_len)
    turns = 2.0 * np.pi * np.outer(np.arange(RADIX), steps) / frames_len
    twiddle = np.stack([np.cos(turns), -np.sin(turns)], axis=1)
    twiddle = np.broadcast_to(twiddle[:, :, None, :], (RADIX, 2, 8, inner))
    return jnp.asarray(table, jnp.bfloat16), jnp.asarray(twiddle, jnp.float32)


def compact_kernel(count_ref, valid_ref, map_ref, frames_ref, out_ref, keep, rows):
    step = pl.program_id(0)
    batch, frame_dev, slots = out_ref.shape
    tile_pix = frames_ref.shape[1] // batch
    per_phase = frame_dev // RADIX
    pitch = RADIX + 1

    @pl.when(step == 0)
    def _():
        row = lax.broadcasted_iota(jnp.int32, (frame_dev, frame_dev), 0)
        col = lax.broadcasted_iota(jnp.int32, (frame_dev, frame_dev), 1)
        source = row % per_phase * RADIX + row // per_phase
        usable = jnp.broadcast_to(valid_ref[...], (frame_dev, frame_dev))
        order = jnp.where(col == source, usable, 0).astype(jnp.float32).astype(jnp.bfloat16)
        ones = jnp.ones((frame_dev, slots), jnp.bfloat16)
        keep[...] = jnp.dot(order, ones, preferred_element_type=jnp.float32)

    pixel = lax.broadcasted_iota(jnp.int32, (tile_pix, slots), 0)
    slot = lax.broadcasted_iota(jnp.int32, (1, slots), 1)
    tiles = lax.broadcasted_iota(jnp.int32, (map_ref.shape[0], slots), 0)
    for which in range(batch):
        tile = step * batch + which
        row = jnp.sum(jnp.where(tiles == tile, map_ref[:, :slots], 0), axis=0, keepdims=True)
        held = jnp.where(slot < count_ref[tile], row, -1)
        hot = jnp.where(jnp.broadcast_to(held, (tile_pix, slots)) == pixel, 1.0, 0.0).astype(jnp.bfloat16)
        block = frames_ref[:, which * tile_pix : (which + 1) * tile_pix]
        picked = jnp.dot(block, hot, preferred_element_type=jnp.float32)
        for part in range(per_phase):
            rows[which, pl.ds(part * pitch, RADIX), :] = picked[part * RADIX : (part + 1) * RADIX, :]
        for phase in range(RADIX):
            span = pl.ds(phase * per_phase, per_phase)
            taken = rows[which, pl.ds(phase, per_phase, stride=pitch), :] * keep[span, :]
            out_ref[which, span, :] = taken.astype(jnp.bfloat16)


def compact(frames, frame_valid, valid_count, block_map):
    frame_dev, pixel_count = frames.shape
    tile_count, tile_pix = block_map.shape
    slots = tile_pix // 2
    batch = 4
    return pl.pallas_call(
        compact_kernel,
        name="compact",
        grid=(tile_count // batch,),
        out_shape=jax.ShapeDtypeStruct((tile_count, frame_dev, slots), jnp.bfloat16),
        in_specs=[
            pl.BlockSpec(memory_space=pltpu.SMEM),
            pl.BlockSpec((1, frame_dev), lambda i: (0, 0)),
            pl.BlockSpec((tile_count, tile_pix), lambda i: (0, 0)),
            pl.BlockSpec((frame_dev, batch * tile_pix), lambda i: (0, i)),
        ],
        out_specs=pl.BlockSpec((batch, frame_dev, slots), lambda i: (i, 0, 0)),
        scratch_shapes=[
            pltpu.VMEM((frame_dev, slots), jnp.float32),
            pltpu.VMEM((batch, frame_dev // RADIX * (RADIX + 1) + 7, slots), jnp.float32),
        ],
    )(valid_count, frame_valid.reshape(1, frame_dev), block_map, frames)


def rotate(real, imag, cos, sin):
    return real * cos - imag * sin, real * sin + imag * cos


def four_point(values):
    (r0, i0), (r1, i1), (r2, i2), (r3, i3) = values
    er, ei, fr, fi = r0 + r2, i0 + i2, r0 - r2, i0 - i2
    gr, gi, hr, hi = r1 + r3, i1 + i3, r1 - r3, i1 - i3
    return [(er + gr, ei + gi), (fr + hi, fi - hr), (er - gr, ei - gi), (fr - hi, fi + hr)]


def sixteen_point_low(values):
    inner = [four_point([values[4 * n + m] for n in range(4)]) for m in range(4)]
    low = [None] * 8
    for k in range(4):
        parts = []
        for m in range(4):
            real, imag = inner[m][k]
            turn = m * k % 16
            if turn == 0:
                parts.append((real, imag))
            elif turn == 4:
                parts.append((imag, -real))
            else:
                angle = -2.0 * math.pi * turn / 16
                parts.append(rotate(real, imag, math.cos(angle), math.sin(angle)))
        (r0, i0), (r1, i1), (r2, i2), (r3, i3) = parts
        low[k] = ((r0 + r2) + (r1 + r3), (i0 + i2) + (i1 + i3))
        low[k + 4] = ((r0 - r2) + (i1 - i3), (i0 - i2) - (r1 - r3))
    return low


def transform_kernel(info_ref, frames_ref, table_ref, twiddle_ref, own_ref, near_ref, far_ref, phases, spread):
    slots = own_ref.shape[0]
    rows = own_ref.shape[1]
    pitch = rows + 1
    half = rows // 2
    inner = table_ref.shape[0]
    places = info_ref.shape[0] - slots - INFO
    width = places // (ROWS + 2 * REACH)
    for phase in range(RADIX):
        if len(frames_ref.shape) == 3:
            per_phase = frames_ref.shape[1] // RADIX
            block = frames_ref[:, phase * per_phase : (phase + 1) * per_phase, :].reshape(inner, slots)
        else:
            block = frames_ref[phase].reshape(inner, slots)
        phases[phase] = lax.dot_general(
            block, table_ref[...], (((0,), (0,)), ((), ())), preferred_element_type=jnp.float32
        )
    chunks = inner // LANES

    def one_group(group, carry):
        first = pl.multiple_of(group * 8, 8)
        for chunk in range(chunks):
            lanes = pl.ds(chunk * LANES, LANES)
            values = []
            for phase in range(RADIX):
                real = phases[phase, pl.ds(first, 8), lanes]
                imag = phases[phase, pl.ds(first, 8), pl.ds(inner + chunk * LANES, LANES)]
                if phase > 0:
                    real, imag = rotate(real, imag, twiddle_ref[phase, 0, :, lanes], twiddle_ref[phase, 1, :, lanes])
                values.append((real, imag))
            for high, (real, imag) in enumerate(sixteen_point_low(values)):
                at = first * pitch + high * chunks + chunk
                spread[pl.ds(at, 8, stride=pitch), :] = real
                spread[pl.ds(at + half, 8, stride=pitch), :] = imag
        return carry

    lax.fori_loop(0, slots // 8, one_group, 0)

    def one_slot(slot, carry):
        own_ref[slot] = spread[pl.ds(slot * pitch, rows), :].astype(jnp.bfloat16)
        return carry

    lax.fori_loop(0, slots, one_slot, 0, unroll=8)
    odd = info_ref[places]
    near_side = jnp.where(odd == 1, 0, width - 3 * REACH)
    far_side = jnp.where(odd == 1, width - 3 * REACH, 0)

    def one_edge(row, carry):
        for column in range(REACH):
            base = (row + REACH) * width + REACH + column
            spot = row * REACH + column
            near_ref[spot] = own_ref[jnp.minimum(info_ref[base + near_side], slots - 1)]
            far_ref[spot] = own_ref[jnp.minimum(info_ref[base + far_side], slots - 1)]
        return carry

    lax.fori_loop(0, ROWS, one_edge, 0, unroll=2)


def transform(info, tile_frames, slots, frames_len):
    table, twiddle = dft_tables(frames_len)
    inner = frames_len // RADIX
    rows = frames_len // LANES
    edge = ROWS * REACH
    whole = pl.BlockSpec(memory_space=pltpu.VMEM)
    return pl.pallas_call(
        transform_kernel,
        name="transform",
        out_shape=(
            jax.ShapeDtypeStruct((slots, rows, LANES), jnp.bfloat16),
            jax.ShapeDtypeStruct((edge, rows, LANES), jnp.bfloat16),
            jax.ShapeDtypeStruct((edge, rows, LANES), jnp.bfloat16),
        ),
        in_specs=[pl.BlockSpec(memory_space=pltpu.SMEM), whole, whole, whole],
        out_specs=(whole, whole, whole),
        scratch_shapes=[
            pltpu.VMEM((RADIX, slots, 2 * inner), jnp.float32),
            pltpu.VMEM((slots * (rows + 1) + 7, LANES), jnp.float32),
        ],
        compiler_params=pltpu.CompilerParams(vmem_limit_bytes=24 * 2**20),
    )(info, tile_frames, table, twiddle)


def inside_kernel(info_ref, own_hbm, out_ref, scale_ref, list_ref, held, *rest):
    totals, (pairs, sem) = rest[:-2], rest[-2:]
    slots, rows, _ = own_hbm.shape
    half = rows // 2
    edge = ROWS * REACH
    places = info_ref.shape[0] - slots - INFO
    width = places // (ROWS + 2 * REACH)
    tile_width = width - 2 * REACH
    empty = slots + 2 * edge
    offsets = len(totals)
    copy = pltpu.make_async_copy(own_hbm, held.at[pl.ds(0, slots)], sem)
    copy.start()
    held[slots] = jnp.zeros((rows, LANES), jnp.bfloat16)
    for total in totals:
        total[...] = jnp.zeros(total.shape, jnp.float32)

    def clear(spot, carry):
        pairs[spot] = 0
        return carry

    lax.fori_loop(0, pairs.shape[0], clear, 0, unroll=8)
    shifts = [info_ref[places + 2 + 2 * j] * width + info_ref[places + 3 + 2 * j] for j in range(offsets)]
    copy.wait()

    def one_slot(slot, listed):
        pixel = info_ref[places + INFO + slot]
        row = pixel // tile_width
        column = pixel % tile_width
        base = (row + REACH) * width + REACH + column
        own_real = held[slot, :half].astype(jnp.float32)
        own_imag = held[slot, half:].astype(jnp.float32)
        for j, total in enumerate(totals):
            other = info_ref[base + shifts[j]]
            at = column * offsets + j
            pairs[at] = pairs[at] + jnp.where(other < empty, 1, 0)
            list_ref[1 + listed] = (at * empty + other) * slots + slot
            listed = listed + jnp.where((other < empty) & (other >= slots), 1, 0)
            within = jnp.minimum(other, slots)
            real = held[within, :half].astype(jnp.float32)
            imag = held[within, half:].astype(jnp.float32)
            total[column, :half] += own_real * real + own_imag * imag
            total[column, half:] += own_imag * real - own_real * imag
        return listed

    list_ref[0] = lax.fori_loop(0, info_ref[places + 1], one_slot, 0)

    def finish(column, carry):
        for j, total in enumerate(totals):
            at = column * offsets + j
            seen = jnp.full((1, LANES), pairs[at], jnp.int32).astype(jnp.float32)
            scaling = 1.0 / jnp.maximum(seen, 1.0)
            scale_ref[pl.ds(at, 1), :] = scaling
            out_ref[at, pl.ds(0, half, stride=2), :] = total[column, :half] * scaling
            out_ref[at, pl.ds(1, half, stride=2), :] = total[column, half:] * scaling
        return carry

    lax.fori_loop(0, tile_width, finish, 0)


def inside(info, own, tile_width, offsets):
    slots, rows, _ = own.shape
    spots = tile_width * offsets
    small = pl.BlockSpec(memory_space=pltpu.SMEM)
    whole = pl.BlockSpec(memory_space=pltpu.VMEM)
    return pl.pallas_call(
        inside_kernel,
        name="inside",
        out_shape=(
            jax.ShapeDtypeStruct((spots, rows, LANES), jnp.float32),
            jax.ShapeDtypeStruct((spots, LANES), jnp.float32),
            jax.ShapeDtypeStruct((slots * offsets + 2,), jnp.int32),
        ),
        in_specs=[small, pl.BlockSpec(memory_space=pl.ANY)],
        out_specs=(whole, whole, small),
        scratch_shapes=[pltpu.VMEM((slots + 1, rows, LANES), jnp.bfloat16)]
        + [pltpu.VMEM((tile_width, rows, LANES), jnp.float32)] * offsets
        + [pltpu.SMEM((spots,), jnp.int32), pltpu.SemaphoreType.DMA],
        compiler_params=pltpu.CompilerParams(vmem_limit_bytes=16 * 2**20),
        cost_estimate=pl.CostEstimate(flops=60_000_000, bytes_accessed=4_000_000, transcendentals=0),
    )(info, own)


def across_kernel(list_ref, scale_ref, own_ref, near_ref, far_ref, part_ref, out_ref):
    slots, rows, _ = own_ref.shape
    edge = near_ref.shape[0]
    half = rows // 2
    empty = slots + 2 * edge
    out_ref[...] = part_ref[...]

    def one_pair(pair, carry):
        code = list_ref[1 + pair]
        slot = code % slots
        other = code // slots % empty - slots
        at = code // slots // empty
        scaling = scale_ref[pl.ds(at, 1), :]
        own_real = own_ref[slot, :half].astype(jnp.float32) * scaling
        own_imag = own_ref[slot, half:].astype(jnp.float32) * scaling
        from_near = other < edge
        close = jnp.minimum(other, edge - 1)
        distant = jnp.maximum(other - edge, 0)
        both = jnp.where(from_near, near_ref[close], far_ref[distant]).astype(jnp.float32)
        real, imag = both[:half], both[half:]
        out_ref[at, pl.ds(0, half, stride=2), :] += own_real * real + own_imag * imag
        out_ref[at, pl.ds(1, half, stride=2), :] += own_imag * real - own_real * imag
        return carry

    lax.fori_loop(0, list_ref[0], one_pair, 0)


def across(listed, scale, own, near, far, part):
    small = pl.BlockSpec(memory_space=pltpu.SMEM)
    whole = pl.BlockSpec(memory_space=pltpu.VMEM)
    return pl.pallas_call(
        across_kernel,
        name="across",
        out_shape=jax.ShapeDtypeStruct(part.shape, part.dtype),
        in_specs=[small, whole, whole, whole, whole, whole],
        out_specs=whole,
        compiler_params=pltpu.CompilerParams(vmem_limit_bytes=16 * 2**20),
    )(listed, scale, own, near, far, part)


def describe(valid_count, block_map, offsets, position):
    tile_pix = block_map.shape[1]
    slots = tile_pix // 2
    tile_width = tile_pix // ROWS
    edge = ROWS * REACH
    empty = slots + 2 * edge
    padded_count = jnp.pad(valid_count, ((1, 1),))
    padded_map = jnp.pad(block_map, ((1, 1), (0, 0)))
    counts = lax.dynamic_slice_in_dim(padded_count, position, 3, 0)
    maps = lax.dynamic_slice_in_dim(padded_map, position, 3, 0)[:, :slots]
    slot_idx = jnp.arange(slots, dtype=jnp.int32)
    pixel_idx = jnp.arange(tile_pix, dtype=jnp.int32)
    match = (maps[:, :, None] == pixel_idx[None, None, :]) & (slot_idx[None, :, None] < counts[:, None, None])
    found = jnp.max(jnp.where(match, slot_idx[None, :, None], -1), axis=1)
    grid = found.reshape(3, ROWS, tile_width)
    spot = (jnp.arange(ROWS, dtype=jnp.int32) * REACH)[:, None] + jnp.arange(REACH, dtype=jnp.int32)[None, :]
    odd = position % 2
    own = jnp.where(grid[1] >= 0, grid[1], empty)
    right = jnp.where(grid[2][:, :REACH] >= 0, slots + odd * edge + spot, empty)
    left = jnp.where(grid[0][:, tile_width - REACH :] >= 0, slots + (1 - odd) * edge + spot, empty)
    place = jnp.concatenate([left, own, right], axis=1)
    place = jnp.pad(place, ((REACH, REACH), (0, 0)), constant_values=empty)
    head = jnp.stack([odd.astype(jnp.int32), counts[1]])
    return jnp.concatenate([place.reshape(-1), head, offsets.reshape(-1), maps[1]])


def per_device(frames, frame_valid, valid_count, block_map, offsets):
    devices = lax.axis_size("tm")
    position = lax.axis_index("tm")
    frame_dev = frames.shape[0]
    frames_len = frame_dev * devices
    tile_pix = block_map.shape[1]
    slots = tile_pix // 2
    tile_width = tile_pix // ROWS
    sent = compact(frames, frame_valid, valid_count, block_map)
    tile_frames = lax.all_to_all(sent, "tm", split_axis=0, concat_axis=0, tiled=True)
    if frame_dev // RADIX % 16 != 0:
        tile_frames = tile_frames.reshape(devices, RADIX, frame_dev // RADIX, slots)
        tile_frames = tile_frames.transpose(1, 0, 2, 3).reshape(RADIX, frames_len // RADIX, slots)
    info = describe(valid_count, block_map, offsets, position)
    own, near, far = transform(info, tile_frames, slots, frames_len)
    far_pairs = [(i, i + 1) for i in range(1, devices - 1, 2)] + [(i + 1, i) for i in range(1, devices - 1, 2)]
    near_pairs = [(i, i + 1) for i in range(0, devices - 1, 2)] + [(i + 1, i) for i in range(0, devices - 1, 2)]
    far = lax.ppermute(far, "tm", far_pairs)
    near = lax.ppermute(near, "tm", near_pairs)
    part, scale, listed = inside(info, own, tile_width, offsets.shape[0])
    result = across(listed, scale, own, near, far, part)
    bins = frames_len // 2
    result = result.reshape(tile_width, offsets.shape[0], bins // LANES, 2, LANES)
    return result.transpose(0, 1, 3, 2, 4).reshape(tile_width, offsets.shape[0], 2, bins)


def solution(mesh):
    return jax.shard_map(
        per_device,
        mesh=mesh,
        in_specs=(P("tm", "groups"), P(("groups", "tm")), P("groups"), P("groups", None), P()),
        out_specs=P(("groups", "tm"), None, None, None),
        check_vma=False,
    )
```

time: 72.2 us -> 58.1 us (0.80)
  waiting for transfers between devices: 34.6 us -> 29.1 us
  local copies, waits for them, and re-layouts: 5.98 us -> 2.01 us
  Pallas kernels: 19.1 us -> 16.6 us
  starting transfers between devices: 10.8 us -> 8.86 us
    ppermute x2, waiting for transfers between devices: 11.5 us -> 6.95 us  [the longest x1 6.94 us: per_device(): far = lax.ppermute(far, 'tm', far_pairs)]
    pallas_call x1, Pallas kernels: 6.63 us -> 3.05 us  [transform(): pl.pallas_call(transform_kernel, name='transform', out_shape=(jax.ShapeDt...]
    unnamed x13 -> x11, local copies, waits for them, and re-layouts: 2.46 us -> 0.12 us
    reshape x2, local copies, waits for them, and re-layouts: 2.01 us -> 0.17 us  [the longest x1 0.09 us: describe(): offsets.reshape(-1)]
    ppermute x2, starting transfers between devices: 4.44 us -> 2.62 us  [the longest x1 2.15 us: per_device(): far = lax.ppermute(far, 'tm', far_pairs)]
    pallas_call x1 -> x2, Pallas kernels: 7.47 us -> 9.1 us  [the longest x1 6.98 us: inside(): pl.pallas_call(inside_kernel, name='inside', out_shape=(jax.ShapeDtypeStr...]
    all_to_all x1, waiting for transfers between devices: 23.1 us -> 22.1 us  [per_device(): lax.all_to_all(sent, 'tm', split_axis=0, concat_axis=0, tiled=True)]
  transfers between devices with their start and end apart: 3 -> 3, of which waited for: 3 -> 2; matrix products, arithmetic and copies ran while one was open for 5% -> 4% of each run, Pallas kernels for 0% -> 12%
where the time goes in v2:
time: 58.1 us; the launch traced here: 57 us
  waiting for transfers between devices  29.1 us (50%)
  Pallas kernels  16.6 us (29%)
  starting transfers between devices  8.86 us (15%)
  local copies, waits for them, and re-layouts  2.01 us (3%)
    all_to_all x1, waiting for transfers between devices, per_device(): lax.all_to_all(sent, 'tm', split_axis=0, concat_axis=0, tiled=True)  22.1 us
    pallas_call x1, Pallas kernels, inside(): pl.pallas_call(inside_kernel, name='inside', out_shape=(jax.ShapeDtypeStr...  6.98 us
    ppermute x1, waiting for transfers between devices, per_device(): far = lax.ppermute(far, 'tm', far_pairs)  6.94 us
    all_to_all x1, starting transfers between devices, per_device(): lax.all_to_all(sent, 'tm', split_axis=0, concat_axis=0, tiled=True)  6.24 us
    pallas_call x1, Pallas kernels, compact(): pl.pallas_call(compact_kernel, name='compact', grid=(tile_count // batch,...  4.43 us
    pallas_call x1, Pallas kernels, transform(): pl.pallas_call(transform_kernel, name='transform', out_shape=(jax.ShapeDt...  3.05 us
    ppermute x1, starting transfers between devices, per_device(): far = lax.ppermute(far, 'tm', far_pairs)  2.15 us
    pallas_call x1, Pallas kernels, across(): pl.pallas_call(across_kernel, name='across', out_shape=jax.ShapeDtypeStru...  2.12 us
  transfers between devices with their start and end apart: 3, of which 2 were waited for; matrix products, arithmetic and copies ran while one was open for 4% of the time, Pallas kernels for 12%

profile of v2, /device:TPU:10, one launch (start us, length us, event | category | flops | bytes accessed | tf_op | source)
XLA Modules:
  0.0 57.0 jit_solution(4564974494440600229)
XLA Ops:
  0.0 0.0 copy-start
  0.0 0.0 copy-start.1
  0.0 4.4 %compact.1 = bf16[16,256,128]{2,1,0:T(8,128)(2,1)} custom-call(s32[16]{0:T(128)} %count_ref.1, s32[1,256]{1,0:T(1,128)} %bitcast.9, s32[16,256]{1,0:T(8,128)} %map_ref.1, bf16[256,4096]{1,0:T(8,128)(2,1)} %frames_ref.1), custom_call_target="tpu_custom_call" | custom-call | tf_op jit(solution)/shard_map/compact/pallas_call | solution.py:70
  4.5 6.2 %all-to-all-start = ((bf16[16,256,128]{2,1,0:T(8,128)(2,1)}), bf16[16,256,128]{2,1,0:T(8,128)(2,1)S(1)}, u32[]{:S(2)}, u32[]{:S(2)}) async-start(bf16[16,256,128]{2,1,0:T(8,128)(2,1)} %compact.1), calls=%async_computation | async-start | bytes 2097152 | tf_op jit(solution)/shard_map/all_to_all | solution.py:360
  10.7 0.1 pad_dynamic-slice_fusion.2
  10.8 0.6 %slice.35 = s32[1]{0:T(128)} slice(s32[3]{0:T(128)S(1)} %pad_dynamic-slice_fusion.2), slice={[1:2]} | slice | bytes 8 | tf_op jit(solution)/shard_map/slice | solution.py:347
  11.4 0.1 copy.12
  11.5 0.1 reshape.53
  11.6 0.1 iota_compare_fusion.1
  11.7 0.2 select_reduce_fusion
  11.9 0.1 squeeze.13
  12.0 0.1 squeeze.15
  12.1 0.1 squeeze.14
  12.2 0.1 add_select_fusion.1
  12.3 0.1 pad_add_fusion
  12.4 0.1 reshape.52
  12.5 0.7 %concatenate.7.info_ref = s32[714]{0:T(1024)S(1)} concatenate(s32[576]{0:T(1024)S(1)} %reshape.52, s32[1]{0:T(128)} %bitcast, s32[1]{0:T(128)} %slice.35, s32[8]{0:T(128)S(1)} %reshape.53, s32[128]{0:T(128)S(1)} %fusion.1), dimensions={0} | concatenate | bytes 5712 | tf_op jit(solution)/shard_map/concatenate | solution.py:348
  13.2 22.1 %all-to-all-done.frames_ref = bf16[16,256,128]{2,1,0:T(8,128)(2,1)S(1)} async-done(((bf16[16,256,128]{2,1,0:T(8,128)(2,1)}), bf16[16,256,128]{2,1,0:T(8,128)(2,1)S(1)}, u32[]{:S(2)}, u32[]{:S(2)}) %all-to-all-start) | async-done | bytes 1048608 | tf_op jit(solution)/shard_map/all_to_all | solution.py:360
  35.3 3.1 %transform.1 = (bf16[128,32,128]{2,1,0:T(8,128)(2,1)S(1)}, bf16[64,32,128]{2,1,0:T(8,128)(2,1)S(1)}, bf16[64,32,128]{2,1,0:T(8,128)(2,1)S(1)}) custom-call(s32[714]{0:T(1024)S(1)} %concatenate.7.info_ref, bf16[16,256,128]{2,1,0:T(8,128)(2,1)S(1)} %all-to-all-done.frames_ref, bf16[256,512]{1,0:T(8,128)(2,1)S(1)} %copy-done.1, f32[16,2,8,256]{3,2,1,0:T(8,128)S(1)} %copy-done), custom_call_target="tpu_custom_call" | custom-call | tf_op jit(solution)/shard_map/transform/pallas_call | solution.py:185
  38.4 0.5 collective-permute-start
  38.8 2.2 %collective-permute-start.1 = (bf16[64,32,128]{2,1,0:T(8,128)(2,1)S(1)}, bf16[64,32,128]{2,1,0:T(8,128)(2,1)S(1)}, u32[]{:S(2)}, u32[]{:S(2)}) collective-permute-start(bf16[64,32,128]{2,1,0:T(8,128)(2,1)S(1)} %get-tuple-element.15), channel_id=1, source_target_pairs={{1,2},{3,4},{5,6},{7,8},{9,10},{11,12},{13,14},{2,1},{4,3},{6,5},{... | collective-permute-start | bytes 1572872 | tf_op jit(solution)/shard_map/ppermute | solution.py:368
  41.0 7.0 %inside.1 = (f32[64,32,128]{2,1,0:T(8,128)S(1)}, f32[64,128]{1,0:T(8,128)S(1)}, s32[514]{0:T(1024)S(1)}) custom-call(s32[714]{0:T(1024)S(1)} %concatenate.7.info_ref, bf16[128,32,128]{2,1,0:T(8,128)(2,1)S(1)} %get-tuple-element.11.own_hbm.own_ref), custom_call_target="tpu_custom_call" | custom-call | flops 60000000 | bytes 4000000 | tf_op jit(solution)/shard_map/inside/pallas_call | solution.py:267
  48.0 6.9 %collective-permute-done.1.far_ref = bf16[64,32,128]{2,1,0:T(8,128)(2,1)S(1)} collective-permute-done((bf16[64,32,128]{2,1,0:T(8,128)(2,1)S(1)}, bf16[64,32,128]{2,1,0:T(8,128)(2,1)S(1)}, u32[]{:S(2)}, u32[]{:S(2)}) %collective-permute-start.1) | collective-permute-done | bytes 524320 | tf_op jit(solution)/shard_map/ppermute | solution.py:368
  54.9 2.1 %across.1 = f32[64,32,128]{2,1,0:T(8,128)} custom-call(s32[514]{0:T(1024)S(1)} %get-tuple-element.12.list_ref, f32[64,128]{1,0:T(8,128)S(1)} %get-tuple-element.13.scale_ref, bf16[128,32,128]{2,1,0:T(8,128)(2,1)S(1)} %get-tuple-element.11.own_hbm.own_ref, bf16[64,32,128]{2,1,0:T(8,128)(2,1)S(1)} %collective-permute-done.near_ref, ...), custom_call_target="tpu_custom_call" | custom-call | tf_op jit(solution)/shard_map/across/pallas_call | solution.py:315
  (15 shorter events, 0.1 us)
Async XLA Ops:
  0.0 10.7 %copy-start.4 = (s32[16]{0:T(128)S(1)}, s32[16]{0:T(128)}, u32[]{:S(2)}) copy-start(s32[16]{0:T(128)} %count_ref.1) | copy-start | bytes 196
  0.0 11.4 %copy-start.3 = (s32[4,2]{0,1:T(2,128)S(1)}, s32[4,2]{0,1:T(2,128)}, u32[]{:S(2)}) copy-start(s32[4,2]{0,1:T(2,128)} %param.11) | copy-start | bytes 100
  0.0 11.6 %copy-start.2 = (s32[16,256]{1,0:T(8,128)S(1)}, s32[16,256]{1,0:T(8,128)}, u32[]{:S(2)}) copy-start(s32[16,256]{1,0:T(8,128)} %map_ref.1) | copy-start | bytes 49156
  0.0 35.3 %copy-start = (f32[16,2,8,256]{3,2,1,0:T(8,128)S(1)}, f32[16,2,8,256]{3,2,1,0:T(8,128)}, u32[]{:S(2)}) copy-start(f32[16,2,8,256]{3,2,1,0:T(8,128)} %constant.40.clone.twiddle_ref) | copy-start | bytes 786436
  0.0 35.3 %copy-start.1 = (bf16[256,512]{1,0:T(8,128)(2,1)S(1)}, bf16[256,512]{1,0:T(8,128)(2,1)}, u32[]{:S(2)}) copy-start(bf16[256,512]{1,0:T(8,128)(2,1)} %constant.39.clone.table_ref) | copy-start | bytes 786436
  4.5 30.8 %all-to-all-start = ((bf16[16,256,128]{2,1,0:T(8,128)(2,1)}), bf16[16,256,128]{2,1,0:T(8,128)(2,1)S(1)}, u32[]{:S(2)}, u32[]{:S(2)}) async-start(bf16[16,256,128]{2,1,0:T(8,128)(2,1)} %compact.1), calls=%async_computation | async-start | bytes 2097152 | tf_op jit(solution)/shard_map/all_to_all | solution.py:360
  38.4 9.6 %collective-permute-start = (bf16[64,32,128]{2,1,0:T(8,128)(2,1)S(1)}, bf16[64,32,128]{2,1,0:T(8,128)(2,1)S(1)}, u32[]{:S(2)}, u32[]{:S(2)}) collective-permute-start(bf16[64,32,128]{2,1,0:T(8,128)(2,1)S(1)} %get-tuple-element.14), channel_id=1, source_target_pairs={{0,1},{2,3},{4,5},{6,7},{8,9},{10,11},{12,13},{14,15},{1,0},{3,2},... | collective-permute-start | bytes 1572872 | tf_op jit(solution)/shard_map/ppermute | solution.py:369
  38.8 16.1 %collective-permute-start.1 = (bf16[64,32,128]{2,1,0:T(8,128)(2,1)S(1)}, bf16[64,32,128]{2,1,0:T(8,128)(2,1)S(1)}, u32[]{:S(2)}, u32[]{:S(2)}) collective-permute-start(bf16[64,32,128]{2,1,0:T(8,128)(2,1)S(1)} %get-tuple-element.15), channel_id=1, source_target_pairs={{1,2},{3,4},{5,6},{7,8},{9,10},{11,12},{13,14},{2,1},{4,3},{6,5},{... | collective-permute-start | bytes 1572872 | tf_op jit(solution)/shard_map/ppermute | solution.py:368

commit v3 on v2

--- a/solution.py
+++ b/solution.py
@@ -27,39 +27,58 @@
     return jnp.asarray(table, jnp.bfloat16), jnp.asarray(twiddle, jnp.float32)
 
 
-def compact_kernel(count_ref, valid_ref, map_ref, frames_ref, out_ref, keep, rows):
-    step = pl.program_id(0)
-    batch, frame_dev, slots = out_ref.shape
-    tile_pix = frames_ref.shape[1] // batch
+def compact_kernel(count_hbm, valid_hbm, map_hbm, frames_hbm, out_hbm, frames, out_ref, keep, rows, count_ref, valid_ref, map_ref, sems, out_sems, small_sems):
+    tile_count, frame_dev, slots = out_ref.shape
+    tile_pix = map_ref.shape[1]
+    batch = frames.shape[2] // tile_pix
     per_phase = frame_dev // RADIX
     pitch = RADIX + 1
-
-    @pl.when(step == 0)
-    def _():
-        row = lax.broadcasted_iota(jnp.int32, (frame_dev, frame_dev), 0)
-        col = lax.broadcasted_iota(jnp.int32, (frame_dev, frame_dev), 1)
-        source = row % per_phase * RADIX + row // per_phase
-        usable = jnp.broadcast_to(valid_ref[...], (frame_dev, frame_dev))
-        order = jnp.where(col == source, usable, 0).astype(jnp.float32).astype(jnp.bfloat16)
-        ones = jnp.ones((frame_dev, slots), jnp.bfloat16)
-        keep[...] = jnp.dot(order, ones, preferred_element_type=jnp.float32)
-
+    copies = []
+    for step in range(frames.shape[0]):
+        span = pl.ds(step * batch * tile_pix, batch * tile_pix)
+        copies.append(pltpu.make_async_copy(frames_hbm.at[:, span], frames.at[step], sems.at[step]))
+        copies[-1].start()
+    smalls = [
+        pltpu.make_async_copy(valid_hbm, valid_ref, small_sems.at[0]),
+        pltpu.make_async_copy(map_hbm, map_ref, small_sems.at[1]),
+        pltpu.make_async_copy(count_hbm, count_ref, small_sems.at[2]),
+    ]
+    for small in smalls:
+        small.start()
+    for small in smalls:
+        small.wait()
+    row = lax.broadcasted_iota(jnp.int32, (frame_dev, frame_dev), 0)
+    col = lax.broadcasted_iota(jnp.int32, (frame_dev, frame_dev), 1)
+    source = row % per_phase * RADIX + row // per_phase
+    usable = jnp.broadcast_to(valid_ref[...], (frame_dev, frame_dev))
+    order = jnp.where(col == source, usable, 0).astype(jnp.float32).astype(jnp.bfloat16)
+    ones = jnp.ones((frame_dev, slots), jnp.bfloat16)
+    keep[...] = jnp.dot(order, ones, preferred_element_type=jnp.float32)
     pixel = lax.broadcasted_iota(jnp.int32, (tile_pix, slots), 0)
     slot = lax.broadcasted_iota(jnp.int32, (1, slots), 1)
-    tiles = lax.broadcasted_iota(jnp.int32, (map_ref.shape[0], slots), 0)
-    for which in range(batch):
+
+    def one_tile(step, which):
         tile = step * batch + which
-        row = jnp.sum(jnp.where(tiles == tile, map_ref[:, :slots], 0), axis=0, keepdims=True)
-        held = jnp.where(slot < count_ref[tile], row, -1)
+        held = jnp.where(slot < count_ref[tile], map_ref[tile : tile + 1, :slots], -1)
         hot = jnp.where(jnp.broadcast_to(held, (tile_pix, slots)) == pixel, 1.0, 0.0).astype(jnp.bfloat16)
-        block = frames_ref[:, which * tile_pix : (which + 1) * tile_pix]
+        block = frames[step, :, which * tile_pix : (which + 1) * tile_pix]
         picked = jnp.dot(block, hot, preferred_element_type=jnp.float32)
         for part in range(per_phase):
             rows[which, pl.ds(part * pitch, RADIX), :] = picked[part * RADIX : (part + 1) * RADIX, :]
         for phase in range(RADIX):
             span = pl.ds(phase * per_phase, per_phase)
             taken = rows[which, pl.ds(phase, per_phase, stride=pitch), :] * keep[span, :]
-            out_ref[which, span, :] = taken.astype(jnp.bfloat16)
+            out_ref[tile, span, :] = taken.astype(jnp.bfloat16)
+
+    for step, copy in enumerate(copies):
+        copy.wait()
+        for which in range(batch):
+            one_tile(step, which)
+        span = pl.ds(step * batch, batch)
+        copies[step] = pltpu.make_async_copy(out_ref.at[span], out_hbm.at[span], out_sems.at[step])
+        copies[step].start()
+    for copy in copies:
+        copy.wait()
 
 
 def compact(frames, frame_valid, valid_count, block_map):
@@ -67,22 +86,27 @@
     tile_count, tile_pix = block_map.shape
     slots = tile_pix // 2
     batch = 4
+    steps = tile_count // batch
+    place = pl.BlockSpec(memory_space=pl.ANY)
     return pl.pallas_call(
         compact_kernel,
         name="compact",
-        grid=(tile_count // batch,),
         out_shape=jax.ShapeDtypeStruct((tile_count, frame_dev, slots), jnp.bfloat16),
-        in_specs=[
-            pl.BlockSpec(memory_space=pltpu.SMEM),
-            pl.BlockSpec((1, frame_dev), lambda i: (0, 0)),
-            pl.BlockSpec((tile_count, tile_pix), lambda i: (0, 0)),
-            pl.BlockSpec((frame_dev, batch * tile_pix), lambda i: (0, i)),
-        ],
-        out_specs=pl.BlockSpec((batch, frame_dev, slots), lambda i: (i, 0, 0)),
+        in_specs=[place] * 4,
+        out_specs=place,
         scratch_shapes=[
+            pltpu.VMEM((steps, frame_dev, batch * tile_pix), jnp.bfloat16),
+            pltpu.VMEM((tile_count, frame_dev, slots), jnp.bfloat16),
             pltpu.VMEM((frame_dev, slots), jnp.float32),
             pltpu.VMEM((batch, frame_dev // RADIX * (RADIX + 1) + 7, slots), jnp.float32),
+            pltpu.SMEM((tile_count,), jnp.int32),
+            pltpu.VMEM((1, frame_dev), jnp.int32),
+            pltpu.VMEM((tile_count, tile_pix), jnp.int32),
+            pltpu.SemaphoreType.DMA((steps,)),
+            pltpu.SemaphoreType.DMA((steps,)),
+            pltpu.SemaphoreType.DMA((3,)),
         ],
+        compiler_params=pltpu.CompilerParams(vmem_limit_bytes=62 * 2**20),
     )(valid_count, frame_valid.reshape(1, frame_dev), block_map, frames)
 
 
@@ -118,14 +142,15 @@
     return low
 
 
-def transform_kernel(info_ref, frames_ref, table_ref, twiddle_ref, own_ref, near_ref, far_ref, phases, spread):
+def transform_kernel(info_ref, frames_ref, table_ref, twiddle_ref, own_ref, *rest):
+    (edges, (phases, spread)) = rest[:-2], rest[-2:]
     slots = own_ref.shape[0]
     rows = own_ref.shape[1]
     pitch = rows + 1
     half = rows // 2
     inner = table_ref.shape[0]
-    places = info_ref.shape[0] - slots - INFO
-    width = places // (ROWS + 2 * REACH)
+    half_edge = ROWS * REACH // 2
+    lists = info_ref.shape[0] - 4 * half_edge
     for phase in range(RADIX):
         if len(frames_ref.shape) == 3:
             per_phase = frames_ref.shape[1] // RADIX
@@ -161,19 +186,13 @@
         return carry
 
     lax.fori_loop(0, slots, one_slot, 0, unroll=8)
-    odd = info_ref[places]
-    near_side = jnp.where(odd == 1, 0, width - 3 * REACH)
-    far_side = jnp.where(odd == 1, width - 3 * REACH, 0)
-
-    def one_edge(row, carry):
-        for column in range(REACH):
-            base = (row + REACH) * width + REACH + column
-            spot = row * REACH + column
-            near_ref[spot] = own_ref[jnp.minimum(info_ref[base + near_side], slots - 1)]
-            far_ref[spot] = own_ref[jnp.minimum(info_ref[base + far_side], slots - 1)]
-        return carry
-
-    lax.fori_loop(0, ROWS, one_edge, 0, unroll=2)
+
+    def one_edge(spot, carry):
+        for part, edge_ref in enumerate(edges):
+            edge_ref[spot] = own_ref[info_ref[lists + part * half_edge + spot]]
+        return carry
+
+    lax.fori_loop(0, half_edge, one_edge, 0, unroll=4)
 
 
 def transform(info, tile_frames, slots, frames_len):
@@ -187,11 +206,10 @@
         name="transform",
         out_shape=(
             jax.ShapeDtypeStruct((slots, rows, LANES), jnp.bfloat16),
-            jax.ShapeDtypeStruct((edge, rows, LANES), jnp.bfloat16),
-            jax.ShapeDtypeStruct((edge, rows, LANES), jnp.bfloat16),
+            *[jax.ShapeDtypeStruct((edge // 2, rows, LANES), jnp.bfloat16)] * 4,
         ),
         in_specs=[pl.BlockSpec(memory_space=pltpu.SMEM), whole, whole, whole],
-        out_specs=(whole, whole, whole),
+        out_specs=(whole,) * 5,
         scratch_shapes=[
             pltpu.VMEM((RADIX, slots, 2 * inner), jnp.float32),
             pltpu.VMEM((slots * (rows + 1) + 7, LANES), jnp.float32),
@@ -205,7 +223,7 @@
     slots, rows, _ = own_hbm.shape
     half = rows // 2
     edge = ROWS * REACH
-    places = info_ref.shape[0] - slots - INFO
+    places = info_ref.shape[0] - slots - INFO - 2 * edge
     width = places // (ROWS + 2 * REACH)
     tile_width = width - 2 * REACH
     empty = slots + 2 * edge
@@ -284,7 +302,8 @@
 
 def across_kernel(list_ref, scale_ref, own_ref, near_ref, far_ref, part_ref, out_ref):
     slots, rows, _ = own_ref.shape
-    edge = near_ref.shape[0]
+    edge = ROWS * REACH
+    sent = near_ref.shape[0]
     half = rows // 2
     empty = slots + 2 * edge
     out_ref[...] = part_ref[...]
@@ -298,7 +317,7 @@
         own_real = own_ref[slot, :half].astype(jnp.float32) * scaling
         own_imag = own_ref[slot, half:].astype(jnp.float32) * scaling
         from_near = other < edge
-        close = jnp.minimum(other, edge - 1)
+        close = jnp.minimum(other, sent - 1)
         distant = jnp.maximum(other - edge, 0)
         both = jnp.where(from_near, near_ref[close], far_ref[distant]).astype(jnp.float32)
         real, imag = both[:half], both[half:]
@@ -323,29 +342,78 @@
 
 
 def describe(valid_count, block_map, offsets, position):
-    tile_pix = block_map.shape[1]
+    tile_count, tile_pix = block_map.shape
     slots = tile_pix // 2
     tile_width = tile_pix // ROWS
     edge = ROWS * REACH
     empty = slots + 2 * edge
-    padded_count = jnp.pad(valid_count, ((1, 1),))
-    padded_map = jnp.pad(block_map, ((1, 1), (0, 0)))
-    counts = lax.dynamic_slice_in_dim(padded_count, position, 3, 0)
-    maps = lax.dynamic_slice_in_dim(padded_map, position, 3, 0)[:, :slots]
+    columns = tile_count * tile_width
     slot_idx = jnp.arange(slots, dtype=jnp.int32)
     pixel_idx = jnp.arange(tile_pix, dtype=jnp.int32)
-    match = (maps[:, :, None] == pixel_idx[None, None, :]) & (slot_idx[None, :, None] < counts[:, None, None])
-    found = jnp.max(jnp.where(match, slot_idx[None, :, None], -1), axis=1)
-    grid = found.reshape(3, ROWS, tile_width)
-    spot = (jnp.arange(ROWS, dtype=jnp.int32) * REACH)[:, None] + jnp.arange(REACH, dtype=jnp.int32)[None, :]
+    held = jnp.where(slot_idx[None, :] < valid_count[:, None], block_map[:, :slots], -1)
+    found = jnp.max(jnp.where(held[:, :, None] == pixel_idx, slot_idx[None, :, None], -1), axis=1)
+    cells = found.reshape(tile_count, ROWS, tile_width)
+    valid = (cells >= 0).astype(jnp.int32)
+    grid = valid.transpose(1, 0, 2).reshape(ROWS, columns)
+    padded = jnp.pad(grid, ((REACH, REACH), (REACH, REACH)))
+    local = jnp.arange(columns, dtype=jnp.int32)[None, :] % tile_width
+    for_left = jnp.zeros_like(grid)
+    for_right = jnp.zeros_like(grid)
+    for j in range(offsets.shape[0]):
+        partner = lax.dynamic_slice(padded, (REACH - offsets[j, 0], REACH - offsets[j, 1]), (ROWS, columns))
+        for_left = jnp.where(local < offsets[j, 1], jnp.maximum(for_left, partner), for_left)
+        for_right = jnp.where(local - offsets[j, 1] >= tile_width, jnp.maximum(for_right, partner), for_right)
+
+    def numbered(needed, first):
+        needed = (needed * grid).reshape(ROWS, tile_count, tile_width)[:, :, first : first + REACH]
+        needed = needed.transpose(1, 0, 2).reshape(tile_count, edge)
+        before = (jnp.arange(edge)[:, None] < jnp.arange(edge)[None, :]).astype(jnp.bfloat16)
+        rank = jnp.dot(needed.astype(jnp.bfloat16), before, preferred_element_type=jnp.float32).astype(jnp.int32)
+        at = cells[:, :, first : first + REACH].reshape(tile_count, edge)
+        return jnp.where(needed > 0, rank, edge), at
+
+    left_rank, left_slot = numbered(for_left, 0)
+    right_rank, right_slot = numbered(for_right, tile_width - REACH)
+    most = jnp.maximum(jnp.max(jnp.where(left_rank < edge, left_rank, -1)), jnp.max(jnp.where(right_rank < edge, right_rank, -1)))
+    few = most < edge // 2
+
+    def own_list(ranks, at):
+        own_rank = lax.dynamic_index_in_dim(ranks, position, 0, keepdims=False)
+        own_at = lax.dynamic_index_in_dim(at, position, 0, keepdims=False)
+        return jnp.max(jnp.where(own_rank[:, None] == jnp.arange(edge)[None, :], own_at[:, None], 0), axis=0)
+
     odd = position % 2
-    own = jnp.where(grid[1] >= 0, grid[1], empty)
-    right = jnp.where(grid[2][:, :REACH] >= 0, slots + odd * edge + spot, empty)
-    left = jnp.where(grid[0][:, tile_width - REACH :] >= 0, slots + (1 - odd) * edge + spot, empty)
-    place = jnp.concatenate([left, own, right], axis=1)
+    left_list = own_list(left_rank, left_slot)
+    right_list = own_list(right_rank, right_slot)
+    near_list = jnp.where(odd == 1, left_list, right_list)
+    far_list = jnp.where(odd == 1, right_list, left_list)
+    above = lax.dynamic_index_in_dim(jnp.pad(left_rank, ((0, 1), (0, 0)), constant_values=edge), position + 1, 0, keepdims=False)
+    below = lax.dynamic_index_in_dim(jnp.pad(right_rank, ((1, 0), (0, 0)), constant_values=edge), position, 0, keepdims=False)
+    right = jnp.where(above < edge, slots + odd * edge + above, empty).reshape(ROWS, REACH)
+    left = jnp.where(below < edge, slots + (1 - odd) * edge + below, empty).reshape(ROWS, REACH)
+    own = lax.dynamic_index_in_dim(cells, position, 0, keepdims=False)
+    place = jnp.concatenate([left, jnp.where(own >= 0, own, empty), right], axis=1)
     place = jnp.pad(place, ((REACH, REACH), (0, 0)), constant_values=empty)
-    head = jnp.stack([odd.astype(jnp.int32), counts[1]])
-    return jnp.concatenate([place.reshape(-1), head, offsets.reshape(-1), maps[1]])
+    own_map = lax.dynamic_index_in_dim(held, position, 0, keepdims=False)
+    own_count = lax.dynamic_index_in_dim(valid_count, position, 0, keepdims=False)
+    head = jnp.stack([odd.astype(jnp.int32), own_count])
+    return jnp.concatenate([place.reshape(-1), head, offsets.reshape(-1), own_map, near_list, far_list]), few
+
+
+def finish_few(operands, near_pairs, far_pairs, tile_width, offsets):
+    info, own, near_a, _, far_a, _ = operands
+    far = lax.ppermute(far_a, "tm", far_pairs)
+    near = lax.ppermute(near_a, "tm", near_pairs)
+    part, scale, listed = inside(info, own, tile_width, offsets)
+    return across(listed, scale, own, near, far, part)
+
+
+def finish_many(operands, near_pairs, far_pairs, tile_width, offsets):
+    info, own, near_a, near_b, far_a, far_b = operands
+    far = lax.ppermute(jnp.concatenate([far_a, far_b]), "tm", far_pairs)
+    near = lax.ppermute(jnp.concatenate([near_a, near_b]), "tm", near_pairs)
+    part, scale, listed = inside(info, own, tile_width, offsets)
+    return across(listed, scale, own, near, far, part)
 
 
 def per_device(frames, frame_valid, valid_count, block_map, offsets):
@@ -361,14 +429,14 @@
     if frame_dev // RADIX % 16 != 0:
         tile_frames = tile_frames.reshape(devices, RADIX, frame_dev // RADIX, slots)
         tile_frames = tile_frames.transpose(1, 0, 2, 3).reshape(RADIX, frames_len // RADIX, slots)
-    info = describe(valid_count, block_map, offsets, position)
-    own, near, far = transform(info, tile_frames, slots, frames_len)
+    info, few = describe(valid_count, block_map, offsets, position)
+    outs = transform(info, tile_frames, slots, frames_len)
     far_pairs = [(i, i + 1) for i in range(1, devices - 1, 2)] + [(i + 1, i) for i in range(1, devices - 1, 2)]
     near_pairs = [(i, i + 1) for i in range(0, devices - 1, 2)] + [(i + 1, i) for i in range(0, devices - 1, 2)]
-    far = lax.ppermute(far, "tm", far_pairs)
-    near = lax.ppermute(near, "tm", near_pairs)
-    part, scale, listed = inside(info, own, tile_width, offsets.shape[0])
-    result = across(listed, scale, own, near, far, part)
+    settings = dict(near_pairs=near_pairs, far_pairs=far_pairs, tile_width=tile_width, offsets=offsets.shape[0])
+    result = lax.cond(
+        few, functools.partial(finish_few, **settings), functools.partial(finish_many, **settings), (info, *outs)
+    )
     bins = frames_len // 2
     result = result.reshape(tile_width, offsets.shape[0], bins // LANES, 2, LANES)
     return result.transpose(0, 1, 3, 2, 4).reshape(tile_width, offsets.shape[0], 2, bins)

time: 58.1 us -> 52.8 us (0.909)
  the two profiles are of different devices: /device:TPU:10 before, /device:TPU:13 now
where the time goes in v3:
time: 52.8 us; the launch traced here: 52.7 us
  Pallas kernels  16 us (30%)
  between operations  11.2 us (21%)
  starting transfers between devices  10 us (19%)
  other arithmetic  6.22 us (12%)
  local copies, waits for them, and re-layouts  5.94 us (11%)
  matrix products  1.74 us (3%)
  waiting for transfers between devices  1.47 us (3%)
    pallas_call x1, Pallas kernels, inside(): pl.pallas_call(inside_kernel, name='inside', out_shape=(jax.ShapeDtypeStr...  8.09 us
    all_to_all x1, starting transfers between devices, per_device(): lax.all_to_all(sent, 'tm', split_axis=0, concat_axis=0, tiled=True)  6.57 us
    pallas_call x1, Pallas kernels, compact(): pl.pallas_call(compact_kernel, name='compact', out_shape=jax.ShapeDtypeSt...  3.52 us
    ppermute x1, starting transfers between devices, finish_few(): far = lax.ppermute(far_a, 'tm', far_pairs)  3.4 us
    pallas_call x1, Pallas kernels, transform(): pl.pallas_call(transform_kernel, name='transform', out_shape=(jax.ShapeDt...  2.96 us
    ge x2, other arithmetic, describe(): local - offsets[j, 1] >= tile_width  2.43 us
    lt x2, other arithmetic, describe(): local < offsets[j, 1]  2.42 us
    dot_general x2, matrix products, numbered(): jnp.dot(needed.astype(jnp.bfloat16), before, preferred_element_type=jnp.f...  1.74 us
  transfers between devices with their start and end apart: 3, of which 1 were waited for; matrix products, arithmetic and copies ran while one was open for 23% of the time, Pallas kernels for 15%

profile of v3, /device:TPU:13, one launch (start us, length us, event | category | flops | bytes accessed | tf_op | source)
XLA Modules:
  0.0 52.7 jit_solution(4358706264557664836)
XLA Ops:
  0.0 3.5 %compact.1 = bf16[16,256,128]{2,1,0:T(8,128)(2,1)} custom-call(s32[16]{0:T(128)} %count_hbm.1, s32[1,256]{1,0:T(1,128)} %bitcast.54, s32[16,256]{1,0:T(8,128)} %map_hbm.1, bf16[256,4096]{1,0:T(8,128)(2,1)} %frames_hbm.1), custom_call_target="tpu_custom_call" | custom-call | tf_op jit(solution)/shard_map/compact/pallas_call | solution.py:91
  3.5 6.6 %all-to-all-start = ((bf16[16,256,128]{2,1,0:T(8,128)(2,1)}), bf16[16,256,128]{2,1,0:T(8,128)(2,1)S(1)}, u32[]{:S(2)}, u32[]{:S(2)}) async-start(bf16[16,256,128]{2,1,0:T(8,128)(2,1)} %compact.1), calls=%async_computation | async-start | bytes 2097152 | tf_op jit(solution)/shard_map/all_to_all | solution.py:428
  10.1 0.7 %fusion.14 = (s32[1,1]{0,1:T(1,128)}, s32[1,1]{0,1:T(1,128)}, s32[1,1]{0,1:T(1,128)}, s32[1,1]{0,1:T(1,128)}, s32[1,1]{0,1:T(1,128)}, /*index=5*/s32[1,1]{0,1:T(1,128)}, s32[1,1]{0,1:T(1,128)}, s32[1,1]{0,1:T(1,128)}) fusion(s32[4,2]{0,1:T(2,128)S(1)} %copy-done.3), kind=kLoop, calls=%fused_computation.65 | loop fusion | bytes 64 | tf_op jit(solution)/shard_map/slice | solution.py:364
  20.5 1.2 %subtract_compare_fusion = (pred[256]{0:T(512)(128)(4,1)S(1)}, pred[256]{0:T(512)(128)(4,1)S(1)}) fusion(s32[]{:T(128)} %bitcast.4, s32[]{:T(128)} %bitcast.3), kind=kLoop, calls=%fused_computation.49 | loop fusion | flops 2560 | bytes 520 | tf_op jit(solution)/shard_map/ge | solution.py:365
  21.7 1.2 %broadcast_compare_fusion = (pred[256]{0:T(512)(128)(4,1)S(1)}, pred[256]{0:T(512)(128)(4,1)S(1)}) fusion(s32[]{:T(128)} %bitcast.4, s32[]{:T(128)} %bitcast.3), kind=kLoop, calls=%fused_computation.60 | loop fusion | flops 2048 | bytes 520 | tf_op jit(solution)/shard_map/lt | solution.py:364
  22.9 1.3 %subtract_compare_fusion.2 = (pred[256]{0:T(512)(128)(4,1)S(1)}, pred[256]{0:T(512)(128)(4,1)S(1)}) fusion(s32[]{:T(128)} %bitcast.2, s32[]{:T(128)} %bitcast.1), kind=kLoop, calls=%fused_computation.51 | loop fusion | flops 2560 | bytes 520 | tf_op jit(solution)/shard_map/ge | solution.py:365
  24.1 1.3 %broadcast_compare_fusion.2 = (pred[256]{0:T(512)(128)(4,1)S(1)}, pred[256]{0:T(512)(128)(4,1)S(1)}) fusion(s32[]{:T(128)} %bitcast.2, s32[]{:T(128)} %bitcast.1), kind=kLoop, calls=%fused_computation.62 | loop fusion | flops 2048 | bytes 520 | tf_op jit(solution)/shard_map/lt | solution.py:364
  25.5 0.5 select_reduce_fusion
  26.9 0.2 copy.34
  27.2 0.8 %fusion.7 = (s32[]{:T(128)}, s32[16,64]{1,0:T(8,128)S(1)}) fusion(pred[16,64]{1,0:T(8,128)(4,1)S(1)} %copy.36, bf16[16,64]{0,1:T(8,128)(2,1)S(1)} %bitcast.53), kind=kOutput, calls=%fused_computation.39 | convolution fusion | flops 140287 | bytes 7172 | tf_op jit(solution)/shard_map/dot_general | solution.py:371
  28.1 0.6 %dynamic_slice.51 = s32[1]{0:T(128)} dynamic-slice(s32[16]{0:T(128)S(1)} %copy-done.4, s32[]{:T(128)S(6)} %select_n.208), dynamic_slice_sizes={1} | dynamic-slice | bytes 12 | tf_op jit(solution)/shard_map/jit(dynamic_index_in_dim)/dynamic_slice | solution.py:398
  29.3 0.2 copy.31
  29.5 0.9 %fusion.6 = (s32[]{:T(128)}, s32[16,64]{1,0:T(8,128)S(1)}) fusion(pred[16,64]{1,0:T(8,128)(4,1)S(1)} %copy.33, bf16[16,64]{0,1:T(8,128)(2,1)S(1)} %bitcast.52), kind=kOutput, calls=%fused_computation.38 | convolution fusion | flops 140287 | bytes 7172 | tf_op jit(solution)/shard_map/dot_general | solution.py:371
  32.1 0.2 copy.39
  32.3 0.2 copy.38
  32.4 0.2 dynamic-slice_reduce_fusion
  32.9 0.7 %concatenate.13.info_ref = s32[842]{0:T(1024)S(1)} concatenate(s32[576]{0:T(1024)S(1)} %reshape.134, s32[1]{0:T(128)} %bitcast.22, s32[1]{0:T(128)} %dynamic_slice.51, s32[8]{0:T(128)S(1)} %reshape.135, s32[128]{0:T(128)S(1)} %fusion.10, s32[64]{0:T(128)S(1)} %get-tuple-element.63, s32[64]{0:T(128)S(1)} %get-tuple-element.62), dimensions={0} | concatenate | bytes 6736 | tf_op jit(solution)/shard_map/concatenate | solution.py:400
  33.6 1.5 %all-to-all-done.frames_ref = bf16[16,256,128]{2,1,0:T(8,128)(2,1)S(1)} async-done(((bf16[16,256,128]{2,1,0:T(8,128)(2,1)}), bf16[16,256,128]{2,1,0:T(8,128)(2,1)S(1)}, u32[]{:S(2)}, u32[]{:S(2)}) %all-to-all-start) | async-done | bytes 1048608 | tf_op jit(solution)/shard_map/all_to_all | solution.py:428
  35.0 3.0 %transform.1 = (bf16[128,32,128]{2,1,0:T(8,128)(2,1)S(1)}, bf16[32,32,128]{2,1,0:T(8,128)(2,1)S(1)}, bf16[32,32,128]{2,1,0:T(8,128)(2,1)S(1)}, bf16[32,32,128]{2,1,0:T(8,128)(2,1)S(1)}, bf16[32,32,128]{2,1,0:T(8,128)(2,1)S(1)}) custom-call(s32[842]{0:T(1024)S(1)} %concatenate.13.info_ref, bf16[16,256,128]{2,1,0:T(8,128)(2,1)S(1)} %all-to-all-done.frames_ref, ...), custom_call_target="tpu_custom_call" | custom-call | tf_op jit(solution)/shard_map/transform/pallas_call | solution.py:204
  38.0 13.0 %conditional.1 = (f32[64,32,128]{2,1,0:T(8,128)S(1)}) conditional(s32[]{:T(128)} %convert_element_type.38, (s32[842]{0:T(1024)S(1)}, bf16[128,32,128]{2,1,0:T(8,128)(2,1)S(1)}, bf16[32,32,128]{2,1,0:T(8,128)(2,1)S(1)}, bf16[32,32,128]{2,1,0:T(8,128)(2,1)S(1)}, bf16[32,32,128]{2,1,0:T(8,128)(2,1)S(1)}, ...), branch_computations={%region_5.6_spmd, %region_6.7_spmd} | conditional | flops 60524288 | bytes 10291544 | solution.py:437
  38.1 3.4 %collective-permute-start.1 = (bf16[32,32,128]{2,1,0:T(8,128)(2,1)S(1)}, bf16[32,32,128]{2,1,0:T(8,128)(2,1)S(1)}, u32[]{:S(2)}, u32[]{:S(2)}) collective-permute-start(bf16[32,32,128]{2,1,0:T(8,128)(2,1)S(1)} %get-tuple-element.42), channel_id=1, source_target_pairs={{1,2},{3,4},{5,6},{7,8},{9,10},{11,12},{13,14},{2,1},{4,3},{6,5},{... | collective-permute-start | bytes 786440 | tf_op jit(solution)/shard_map/cond/branch_1_fun/ppermute | solution.py:405
  41.5 8.1 %inside.3 = (f32[64,32,128]{2,1,0:T(8,128)S(1)}, f32[64,128]{1,0:T(8,128)S(1)}, s32[514]{0:T(1024)S(1)}) custom-call(s32[842]{0:T(1024)S(1)} %get-tuple-element.37.info_ref, bf16[128,32,128]{2,1,0:T(8,128)(2,1)S(1)} %get-tuple-element.38.own_hbm.own_ref), custom_call_target="tpu_custom_call" | custom-call | flops 60000000 | bytes 4000000 | tf_op jit(solution)/shard_map/cond/branch_1_fun/inside/pallas_call | solution.py:285
  49.6 1.4 %across.3 = f32[64,32,128]{2,1,0:T(8,128)S(1)} custom-call(s32[514]{0:T(1024)S(1)} %get-tuple-element.39.list_ref, f32[64,128]{1,0:T(8,128)S(1)} %get-tuple-element.40.scale_ref, bf16[128,32,128]{2,1,0:T(8,128)(2,1)S(1)} %get-tuple-element.38.own_hbm.own_ref, bf16[32,32,128]{2,1,0:T(8,128)(2,1)S(1)} %collective-permute-done.near_ref, ...), custom_call_target="tpu_custom_call" | custom-call | tf_op jit(solution)/shard_map/cond/branch_1_fun/across/pallas_call | solution.py:334
  51.2 1.5 %reshape.140 = f32[16,4,2,2048]{3,2,1,0:T(2,128)} reshape(f32[16,4,2,16,128]{4,3,2,1,0:T(8,128)S(1)} %bitcast.47) | data formatting | bytes 2097152 | tf_op jit(solution)/shard_map/reshape | solution.py:442
  (46 shorter events, 2.5 us)
Async XLA Ops:
  0.0 10.1 %copy-start.3 = (s32[4,2]{0,1:T(2,128)S(1)}, s32[4,2]{0,1:T(2,128)}, u32[]{:S(2)}) copy-start(s32[4,2]{0,1:T(2,128)} %param.13) | copy-start | bytes 100
  0.0 25.4 %copy-start.2 = (s32[16,256]{1,0:T(8,128)S(1)}, s32[16,256]{1,0:T(8,128)}, u32[]{:S(2)}) copy-start(s32[16,256]{1,0:T(8,128)} %map_hbm.1) | copy-start | bytes 49156
  0.0 25.4 %copy-start.4 = (s32[16]{0:T(128)S(1)}, s32[16]{0:T(128)}, u32[]{:S(2)}) copy-start(s32[16]{0:T(128)} %count_hbm.1) | copy-start | bytes 196
  3.5 31.5 %all-to-all-start = ((bf16[16,256,128]{2,1,0:T(8,128)(2,1)}), bf16[16,256,128]{2,1,0:T(8,128)(2,1)S(1)}, u32[]{:S(2)}, u32[]{:S(2)}) async-start(bf16[16,256,128]{2,1,0:T(8,128)(2,1)} %compact.1), calls=%async_computation | async-start | bytes 2097152 | tf_op jit(solution)/shard_map/all_to_all | solution.py:428
  10.1 24.9 %copy-start = (f32[16,2,8,256]{3,2,1,0:T(8,128)S(1)}, f32[16,2,8,256]{3,2,1,0:T(8,128)}, u32[]{:S(2)}) copy-start(f32[16,2,8,256]{3,2,1,0:T(8,128)} %constant.116.clone.twiddle_ref) | copy-start | bytes 786436
  10.1 24.9 %copy-start.1 = (bf16[256,512]{1,0:T(8,128)(2,1)S(1)}, bf16[256,512]{1,0:T(8,128)(2,1)}, u32[]{:S(2)}) copy-start(bf16[256,512]{1,0:T(8,128)(2,1)} %constant.115.clone.table_ref) | copy-start | bytes 786436
  38.0 11.6 %collective-permute-start = (bf16[32,32,128]{2,1,0:T(8,128)(2,1)S(1)}, bf16[32,32,128]{2,1,0:T(8,128)(2,1)S(1)}, u32[]{:S(2)}, u32[]{:S(2)}) collective-permute-start(bf16[32,32,128]{2,1,0:T(8,128)(2,1)S(1)} %get-tuple-element.41), channel_id=1, source_target_pairs={{0,1},{2,3},{4,5},{6,7},{8,9},{10,11},{12,13},{14,15},{1,0},{3,2},... | collective-permute-start | bytes 786440 | tf_op jit(solution)/shard_map/cond/branch_1_fun/ppermute | solution.py:406
  38.1 11.5 %collective-permute-start.1 = (bf16[32,32,128]{2,1,0:T(8,128)(2,1)S(1)}, bf16[32,32,128]{2,1,0:T(8,128)(2,1)S(1)}, u32[]{:S(2)}, u32[]{:S(2)}) collective-permute-start(bf16[32,32,128]{2,1,0:T(8,128)(2,1)S(1)} %get-tuple-element.42), channel_id=1, source_target_pairs={{1,2},{3,4},{5,6},{7,8},{9,10},{11,12},{13,14},{2,1},{4,3},{6,5},{... | collective-permute-start | bytes 786440 | tf_op jit(solution)/shard_map/cond/branch_1_fun/ppermute | solution.py:405
